TPU v7x, 32 devices: a whole 2x2x4 slice. The times are simulated.
32 devices in a mesh: mem: 2 (over y), row: 4 (over x, core), col: 4 (over z).
Axes of the slice: x: 2, y: 2, z: 4, core: 2. Of those that a mesh axis runs over, the one named last changes fastest.
Arguments:
- background_sample: float32 [64, 4, 32, 32, 512], P('mem', None, None, 'row', 'col'), may hold values from -6 to 6
- coupling: float32 [4, 4], replicated, may hold values from -0.6 to 0.6
- diffusion: float32 [32], replicated, may hold values from 0.02 to 0.12
- wind_row: float32 [32], replicated, may hold values from -0.4 to 0.4
- wind_col: float32 [32], replicated, may hold values from -0.4 to 0.4
- observed_entry_index: int32 [64, 32, 512], P(None, 'row', ('col', 'mem')), may hold values from 0 to 127
- obs_value: float32 [64, 32, 512], P(None, 'row', ('col', 'mem')), may hold values from -6 to 6
- obs_weight: float32 [64, 32, 512], P(None, 'row', ('col', 'mem')), may hold values from 0.25 to 4
Outputs:
- analysis: float32 [64, 4, 32, 32, 512], P(None, None, None, 'row', ('col', 'mem'))
Inputs may be any that keep to these rules, and one draw needn't show every extreme that they name: observed_entry_index names an entry of a column as variable times 32 plus level.
All inputs are finite; a program needn't handle non-finite values.
Results may differ from a plain program's by a relative error of at most 0.0003.
Values sent between devices are 32-bit elements; how exact they have to be, the bound alone decides.
A program may use at most 256 MiB of HBM per device.

v0:
```python
import jax
import jax.numpy as jnp
from jax import lax
from jax.sharding import PartitionSpec as P

STEPS = 2
NS_ITERS = 2


def extended(value, sides, width):
    for axis, dim in sides:
        count, length = (lax.axis_size(axis), value.shape[dim])
        up = [(i, (i + 1) % count) for i in range(count - 1)]
        down = [(j, i) for i, j in up]
        last = lax.slice_in_dim(value, length - width, length, axis=dim)
        first = lax.slice_in_dim(value, 0, width, axis=dim)
        before = lax.ppermute(last, axis, up)
        after = lax.ppermute(first, axis, down)
        value = jnp.concatenate([before, value, after], axis=dim)
    return value


def tendency(padded, diffusion, wind_row, wind_col, coupling):
    centre = padded[..., 1:-1, 1:-1]
    north = padded[..., :-2, 1:-1]
    south = padded[..., 2:, 1:-1]
    west = padded[..., 1:-1, :-2]
    east = padded[..., 1:-1, 2:]
    ensemble_spread = north + south + west + east - 4.0 * centre
    mixed = jnp.einsum("vw,...wlij->...vlij", coupling, centre, precision=lax.Precision.HIGHEST)
    return (
        diffusion[:, None, None] * ensemble_spread
        - 0.5 * wind_row[:, None, None] * (south - north)
        - 0.5 * wind_col[:, None, None] * (east - west)
        + mixed
    )


def rimmed(field):
    return extended(field, (("row", 3), ("col", 4)), 1)


def begin(state):
    return (state, 0)


def propagate_model(state, margin_width, diffusion, wind_row, wind_col, coupling):
    first = tendency(rimmed(state), diffusion, wind_row, wind_col, coupling)
    middle = state + first
    second = tendency(rimmed(middle), diffusion, wind_row, wind_col, coupling)
    return (state + 0.5 * (first + second), margin_width)


def analyse(block, index, value, weight):
    members = block.shape[0]
    entries = block.shape[1]
    highest = lax.Precision.HIGHEST
    mean = jnp.mean(block, axis=0)
    pert = block - mean[None]
    onehot = (index[:, None, :] == jnp.arange(entries, dtype=jnp.int32)[None, :, None]).astype(
        jnp.float32
    )
    measurement_data = jnp.einsum("mvc,kvc->mkc", block, onehot, precision=highest)
    obs_mean = jnp.mean(measurement_data, axis=0)
    obs_pert = measurement_data - obs_mean[None]
    scaled = obs_pert * weight[None]
    eye = jnp.eye(members, dtype=jnp.float32)[:, :, None]
    system = jnp.einsum("mkc,nkc->mnc", scaled, obs_pert, precision=highest) + (members - 1.0) * eye
    scale = jnp.sqrt(jnp.sum(system * system, axis=(0, 1)))
    current = system / scale[None, None]
    inverse = jnp.broadcast_to(eye, system.shape)
    for sweep in range(NS_ITERS):
        factor = 1.5 * eye - 0.5 * jnp.einsum("mjc,jnc->mnc", inverse, current, precision=highest)
        current = jnp.einsum("mjc,jnc->mnc", current, factor, precision=highest)
        inverse = jnp.einsum("mjc,jnc->mnc", factor, inverse, precision=highest)
    gain_vec = jnp.einsum("mkc,kc->mc", scaled, value - obs_mean, precision=highest)
    half_vec = jnp.einsum("mjc,jc->mc", inverse, gain_vec, precision=highest)
    centre = jnp.einsum("mjc,jc->mc", inverse, half_vec, precision=highest) / scale[None]
    analysis_coefficients = (
        inverse * jnp.sqrt((members - 1.0) / scale)[None, None] + centre[:, None, :]
    )
    return mean[None] + jnp.einsum("mvc,mnc->nvc", pert, analysis_coefficients, precision=highest)


def body(
    background_sample,
    coupling,
    diffusion,
    wind_row,
    wind_col,
    observed_entry_index,
    obs_value,
    obs_weight,
):
    state, margin_width = begin(background_sample)
    for step in range(STEPS):
        state, margin_width = propagate_model(
            state, margin_width, diffusion, wind_row, wind_col, coupling
        )
    moved = lax.all_to_all(state, "mem", split_axis=4, concat_axis=0, tiled=True)
    members, variables, levels, rows_local, cols_local = moved.shape
    cells = rows_local * cols_local
    flat = moved.reshape(members, variables * levels, cells)
    observations = observed_entry_index.shape[0]
    result = analyse(
        flat,
        observed_entry_index.reshape(observations, cells),
        obs_value.reshape(observations, cells),
        obs_weight.reshape(observations, cells),
    )
    return result.reshape(members, variables, levels, rows_local, cols_local)


def solution(mesh):
    placed = (
        P("mem", None, None, "row", "col"),
        P(),
        P(),
        P(),
        P(),
        P(None, "row", ("col", "mem")),
        P(None, "row", ("col", "mem")),
        P(None, "row", ("col", "mem")),
    )
    return jax.shard_map(
        body,
        mesh=mesh,
        in_specs=placed,
        out_specs=P(None, None, None, "row", ("col", "mem")),
        check_vma=False,
    )
```

profile of v0, /device:TPU:25, one launch (start us, length us, event | category | flops | bytes accessed | tf_op | source)
XLA Modules:
  0.0 1773.8 jit_solution(5776532296500759615)
XLA Ops:
  0.0 19.3 %copy.101 = f32[32,4,32,8,128]{4,1,3,2,0:T(4,128)S(1)} copy(f32[32,4,32,8,128]{4,3,2,1,0:T(8,128)} %param.8) | data formatting | bytes 33554432 | tf_op args[0]
  28.4 21.3 %collective-permute-done = f32[32,4,32,1,128]{4,1,3,2,0:T(4,128)S(1)} collective-permute-done((f32[32,4,32,1,128]{4,1,3,2,0:T(4,128)}, f32[32,4,32,1,128]{4,1,3,2,0:T(4,128)S(1)}, u32[]{:S(2)}, u32[]{:S(2)}) %collective-permute-start) | collective-permute-done | bytes 2097184 | tf_op jit(solution)/shard_map/ppermute | solution.py:17
  65.9 28.9 %fusion.70 = (f32[32,4,32,10,1]{4,1,3,2,0:T(4,128)}, f32[32,4,32,10,1]{4,1,3,2,0:T(4,128)}) fusion(f32[32,4,32,10,128]{4,1,3,2,0:T(4,128)} %constant_dynamic-update-slice_fusion), kind=kLoop, calls=%fused_computation.116 | loop fusion | bytes 655360 | tf_op jit(solution)/shard_map/slice | solution.py:15
  94.8 17.9 %copy.90 = f32[32,4,32,10,1]{2,0,4,3,1:T(8,128)S(1)} copy(f32[32,4,32,10,1]{4,1,3,2,0:T(4,128)} %get-tuple-element.11) | data formatting | bytes 327680 | tf_op jit(solution)/shard_map/slice | solution.py:15
  114.0 18.7 %copy.92 = f32[32,4,32,10,1]{2,0,4,3,1:T(8,128)} copy(f32[32,4,32,10,1]{4,1,3,2,0:T(4,128)} %get-tuple-element.12) | data formatting | bytes 327680 | tf_op jit(solution)/shard_map/slice | solution.py:16
  138.1 15.7 copy.91
  153.8 16.8 copy.93
  170.6 81.6 %copy_add_fusion = (f32[32,4,32,8,128]{4,1,3,2,0:T(4,128)}, f32[32,4,32,8,128]{4,1,3,2,0:T(4,128)}) fusion(f32[32,4,32,8,128]{4,3,2,1,0:T(8,128)} %param.8, f32[32,4,32,8,128]{4,1,3,2,0:T(4,128)} %copy-done.3, f32[4,4]{1,0:T(4,128)S(1)} %copy-done, f32[32]{0:T(128)S(1)} %get-tuple-element.33, f32[32]{0:T(128)S(1)} %get-tuple-element.34, ...), kind=kOutput, calls=%fused_computation.112 | convolution fusion | flops 276824064 | bytes 92602816 | tf_op jit(solution)/shard_map/vw,...wlij->...vlij/dot_general | solution.py:30
  261.7 21.0 %collective-permute-done.4 = f32[32,4,32,1,128]{4,1,3,2,0:T(4,128)S(1)} collective-permute-done((f32[32,4,32,1,128]{4,1,3,2,0:T(4,128)S(1)}, f32[32,4,32,1,128]{4,1,3,2,0:T(4,128)S(1)}, u32[]{:S(2)}, u32[]{:S(2)}) %collective-permute-start.4) | collective-permute-done | bytes 2097184 | tf_op jit(solution)/shard_map/ppermute | solution.py:17
  288.4 20.3 %pad_maximum_fusion = f32[32,4,32,10,128]{4,1,3,2,0:T(4,128)} fusion(f32[32,4,32,1,128]{4,1,3,2,0:T(4,128)S(1)} %collective-permute-done.5, f32[32,4,32,8,128]{4,1,3,2,0:T(4,128)} %get-tuple-element.25, f32[32,4,32,1,128]{4,1,3,2,0:T(4,128)S(1)} %collective-permute-done.4), kind=kLoop, calls=%fused_computation.4 | loop fusion | flops 10485760 | bytes 41943040 | tf_op jit(solution)/shard_map/concatenate | solution.py:19
  308.8 29.0 %fusion.69 = (f32[32,4,32,10,1]{4,1,3,2,0:T(4,128)}, f32[32,4,32,10,1]{4,1,3,2,0:T(4,128)}) fusion(f32[32,4,32,10,128]{4,1,3,2,0:T(4,128)} %pad_maximum_fusion), kind=kLoop, calls=%fused_computation.115 | loop fusion | bytes 655360 | tf_op jit(solution)/shard_map/slice | solution.py:15
  337.8 17.8 %copy.99 = f32[32,4,32,10,1]{2,0,4,3,1:T(8,128)S(1)} copy(f32[32,4,32,10,1]{4,1,3,2,0:T(4,128)} %get-tuple-element.10) | data formatting | bytes 327680 | tf_op jit(solution)/shard_map/slice | solution.py:16
  356.9 18.7 %copy.97 = f32[32,4,32,10,1]{2,0,4,3,1:T(8,128)} copy(f32[32,4,32,10,1]{4,1,3,2,0:T(4,128)} %get-tuple-element.9) | data formatting | bytes 327680 | tf_op jit(solution)/shard_map/slice | solution.py:15
  391.9 16.8 copy.98
  408.7 82.9 %fusion.21 = f32[32,4,32,8,128]{4,1,3,2,0:T(4,128)} fusion(f32[32,4,32,8,128]{4,1,3,2,0:T(4,128)} %get-tuple-element.26, f32[32,4,32,8,128]{4,1,3,2,0:T(4,128)} %get-tuple-element.25, f32[32,4,32,10,1]{4,1,3,2,0:T(4,128)} %copy.100, f32[32,4,32,1,128]{4,1,3,2,0:T(4,128)} %copy-done.5, f32[32,4,32,1,128]{4,1,3,2,0:T(4,128)S(1)} %collective-permute-done.4, ...), kind=kOutput, calls=%fused_computation.61 | convolution fusion | flops 301989888 | bytes 71631296 | tf_op jit(solution)/shard_map/vw,...wlij->...vlij/dot_general | solution.py:30
  498.8 20.5 %collective-permute-done.8 = f32[32,4,32,1,128]{4,1,3,2,0:T(4,128)S(1)} collective-permute-done((f32[32,4,32,1,128]{4,1,3,2,0:T(4,128)S(1)}, f32[32,4,32,1,128]{4,1,3,2,0:T(4,128)S(1)}, u32[]{:S(2)}, u32[]{:S(2)}) %collective-permute-start.8) | collective-permute-done | bytes 2097184 | tf_op jit(solution)/shard_map/ppermute | solution.py:17
  525.0 20.3 %pad_maximum_fusion.1 = f32[32,4,32,10,128]{4,1,3,2,0:T(4,128)} fusion(f32[32,4,32,1,128]{4,1,3,2,0:T(4,128)S(1)} %collective-permute-done.9, f32[32,4,32,8,128]{4,1,3,2,0:T(4,128)} %fusion.21, f32[32,4,32,1,128]{4,1,3,2,0:T(4,128)S(1)} %collective-permute-done.8), kind=kLoop, calls=%fused_computation.5 | loop fusion | flops 10485760 | bytes 41943040 | tf_op jit(solution)/shard_map/concatenate | solution.py:19
  545.3 28.9 %fusion.68 = (f32[32,4,32,10,1]{4,1,3,2,0:T(4,128)}, f32[32,4,32,10,1]{4,1,3,2,0:T(4,128)}) fusion(f32[32,4,32,10,128]{4,1,3,2,0:T(4,128)} %pad_maximum_fusion.1), kind=kLoop, calls=%fused_computation.114 | loop fusion | bytes 655360 | tf_op jit(solution)/shard_map/slice | solution.py:15
  574.3 17.8 %copy.102 = f32[32,4,32,10,1]{2,0,4,3,1:T(8,128)S(1)} copy(f32[32,4,32,10,1]{4,1,3,2,0:T(4,128)} %get-tuple-element.7) | data formatting | bytes 327680 | tf_op jit(solution)/shard_map/slice | solution.py:15
  593.4 18.7 %copy.104 = f32[32,4,32,10,1]{2,0,4,3,1:T(8,128)} copy(f32[32,4,32,10,1]{4,1,3,2,0:T(4,128)} %get-tuple-element.8) | data formatting | bytes 327680 | tf_op jit(solution)/shard_map/slice | solution.py:16
  633.8 16.1 copy.105
  649.9 80.2 %fusion.75 = (f32[32,4,32,8,128]{4,1,3,2,0:T(4,128)}, f32[32,4,32,8,128]{4,1,3,2,0:T(4,128)}) fusion(f32[32,4,32,8,128]{4,1,3,2,0:T(4,128)} %fusion.21, f32[4,4]{1,0:T(4,128)S(1)} %copy-done, f32[32]{0:T(128)S(1)} %get-tuple-element.33, f32[32]{0:T(128)S(1)} %get-tuple-element.34, f32[32,4,32,10,1]{4,1,3,2,0:T(4,128)} %copy.105, ...), kind=kOutput, calls=%fused_computation.121 | convolution fusion | flops 293601280 | bytes 54854080 | tf_op jit(solution)/shard_map/vw,...wlij->...vlij/dot_general | solution.py:30
  737.2 20.5 %collective-permute-done.12 = f32[32,4,32,1,128]{4,1,3,2,0:T(4,128)S(1)} collective-permute-done((f32[32,4,32,1,128]{4,1,3,2,0:T(4,128)S(1)}, f32[32,4,32,1,128]{4,1,3,2,0:T(4,128)S(1)}, u32[]{:S(2)}, u32[]{:S(2)}) %collective-permute-start.12) | collective-permute-done | bytes 2097184 | tf_op jit(solution)/shard_map/ppermute | solution.py:17
  763.5 20.3 %pad_maximum_fusion.2 = f32[32,4,32,10,128]{4,1,3,2,0:T(4,128)} fusion(f32[32,4,32,1,128]{4,1,3,2,0:T(4,128)S(1)} %collective-permute-done.13, f32[32,4,32,8,128]{4,1,3,2,0:T(4,128)} %get-tuple-element.27, f32[32,4,32,1,128]{4,1,3,2,0:T(4,128)S(1)} %collective-permute-done.12), kind=kLoop, calls=%fused_computation.6 | loop fusion | flops 10485760 | bytes 41943040 | tf_op jit(solution)/shard_map/concatenate | solution.py:19
  783.8 29.0 %fusion.67 = (f32[32,4,32,10,1]{4,1,3,2,0:T(4,128)}, f32[32,4,32,10,1]{4,1,3,2,0:T(4,128)}) fusion(f32[32,4,32,10,128]{4,1,3,2,0:T(4,128)} %pad_maximum_fusion.2), kind=kLoop, calls=%fused_computation.113 | loop fusion | bytes 655360 | tf_op jit(solution)/shard_map/slice | solution.py:15
  812.8 17.9 %copy.106 = f32[32,4,32,10,1]{2,0,4,3,1:T(8,128)S(1)} copy(f32[32,4,32,10,1]{4,1,3,2,0:T(4,128)} %get-tuple-element.5) | data formatting | bytes 327680 | tf_op jit(solution)/shard_map/slice | solution.py:15
  832.0 18.7 %copy.108 = f32[32,4,32,10,1]{2,0,4,3,1:T(8,128)} copy(f32[32,4,32,10,1]{4,1,3,2,0:T(4,128)} %get-tuple-element.6) | data formatting | bytes 327680 | tf_op jit(solution)/shard_map/slice | solution.py:16
  871.6 16.1 copy.109
  887.7 76.9 %fusion.18 = f32[32,4,32,8,128]{4,1,3,2,0:T(4,128)} fusion(f32[32,4,32,8,128]{4,1,3,2,0:T(4,128)} %fusion.21, f32[32,4,32,8,128]{4,1,3,2,0:T(4,128)} %get-tuple-element.28, f32[32,4,32,8,128]{4,1,3,2,0:T(4,128)} %get-tuple-element.27, f32[32,4,32,10,1]{4,1,3,2,0:T(4,128)} %copy.109, f32[32,4,32,1,128]{4,1,3,2,0:T(4,128)} %copy-done.4, ...), kind=kOutput, calls=%fused_computation.56 | convolution fusion | flops 301989888 | bytes 71631296 | tf_op jit(solution)/shard_map/vw,...wlij->...vlij/dot_general | solution.py:30
  964.5 50.7 %copy.110 = f32[32,4,32,8,128]{2,3,1,0,4:T(8,128)} copy(f32[32,4,32,8,128]{4,1,3,2,0:T(4,128)} %fusion.18) | data formatting | bytes 33554432 | tf_op jit(solution)/shard_map/add | solution.py:51
  1015.3 60.8 %reshape.73 = f32[2,1,2097152]{2,1,0:T(1,128)} reshape(f32[128,32,4,8,32]{4,3,2,1,0:T(8,128)} %bitcast.116) | data formatting | bytes 33554432
  1086.4 162.2 %all-to-all-done = f32[2,1,2097152]{2,1,0:T(1,128)} async-done(((f32[2,1,2097152]{2,1,0:T(1,128)}), f32[2,1,2097152]{2,1,0:T(1,128)}, u32[]{:S(2)}, u32[]{:S(2)}) %all-to-all-start) | async-done | bytes 16777248 | tf_op jit(solution)/shard_map/all_to_all | solution.py:100
  1249.2 61.0 %reduce.1 = f32[2,2097152]{1,0:T(2,128)} reduce(f32[2,1,2097152]{2,1,0:T(1,128)} %all-to-all-done, f32[]{:T(128)} %broadcast.90), dimensions={1}, to_apply=%all_to_all.11.reduce_sub_computation | reduce | bytes 33554436 | tf_op jit(solution)/shard_map/all_to_all | solution.py:100
  1310.2 64.8 %reshape.74 = f32[128,32,4,8,32]{4,3,2,1,0:T(8,128)} reshape(f32[2,2097152]{1,0:T(2,128)} %reduce.1) | data formatting | bytes 33554432
  1375.0 53.7 %copy.111 = f32[32,4,32,8,2,64]{5,3,2,1,0,4:T(8,128)} copy(f32[32,4,32,8,2,64]{2,3,1,0,5,4:T(8,128)} %bitcast.7) | data formatting | bytes 33554432 | tf_op jit(solution)/shard_map/all_to_all | solution.py:100
  1428.8 27.6 %reshape.63 = f32[64,128,512]{2,1,0:T(8,128)} reshape(f32[2,32,4,32,8,64]{5,4,3,2,1,0:T(8,128)} %bitcast.134) | data formatting | bytes 33554432 | tf_op jit(solution)/shard_map/reshape | solution.py:103
  1456.4 16.5 copy.114
  1472.9 21.5 %bitcast_reduce_fusion = (f32[64,512]{0,1:T(8,128)S(1)}, f32[512,64,64]{1,2,0:T(8,128)S(1)}) fusion(f32[64,128,512]{1,0,2:T(8,128)} %copy.114, s32[64,512]{0,1:T(8,128)S(1)} %bitcast.139), kind=kOutput, calls=%fused_computation.52 | convolution fusion | flops 3227484160 | bytes 25427968 | tf_op jit(solution)/shard_map/mvc,kvc->mkc/dot_general | solution.py:63
  1494.5 31.5 %multiply_reduce_fusion = (f32[512]{0:T(512)S(1)}, f32[512,64,64]{2,1,0:T(8,128)}) fusion(f32[64,64]{0,1:T(8,128)S(1)} %get-tuple-element.35, f32[512,64,64]{1,2,0:T(8,128)S(1)} %get-tuple-element.30, f32[64,512]{0,1:T(8,128)S(1)} %bitcast.137, f32[64,512]{0,1:T(8,128)S(1)} %get-tuple-element.22), kind=kOutput, calls=%fused_computation.65 | convolution fusion | flops 1623195136 | bytes 17057792 | tf_op jit(solution)/shard_map/mkc,nkc->mnc/dot_general | solution.py:68
  1525.9 20.7 %fusion.46 = f32[512,64,64]{2,1,0:T(8,128)} fusion(f32[64,64]{0,1:T(8,128)S(1)} %fusion.59, f32[512,64,64]{2,1,0:T(8,128)} %get-tuple-element.32, f32[512]{0:T(512)S(1)} %get-tuple-element.24, f32[64,64]{0,1:T(8,128)S(1)} %get-tuple-element.35), kind=kOutput, calls=%fused_computation.85 | convolution fusion | flops 1614807040 | bytes 16812032 | tf_op jit(solution)/shard_map/mjc,jnc->mnc/dot_general | solution.py:73
  1546.6 25.4 %fusion.26 = f32[512,64,64]{2,1,0:T(8,128)} fusion(f32[512,64,64]{2,1,0:T(8,128)} %fusion.46, f32[64,64]{0,1:T(8,128)S(1)} %get-tuple-element.36, f32[512,64,64]{2,1,0:T(8,128)} %get-tuple-element.32, f32[512]{0:T(512)S(1)} %get-tuple-element.24, f32[64,64]{0,1:T(8,128)S(1)} %get-tuple-element.35), kind=kOutput, calls=%fused_computation.69 | convolution fusion | flops 1619001344 | bytes 25200640 | tf_op jit(solution)/shard_map/mjc,jnc->mnc/dot_general | solution.py:74
  1572.0 19.8 %fusion.27 = f32[512,64,64]{2,1,0:T(8,128)} fusion(f32[512,64,64]{2,1,0:T(8,128)} %fusion.46, f32[64,64]{0,1:T(8,128)S(1)} %get-tuple-element.36, f32[64,64]{0,1:T(8,128)S(1)} %fusion.59), kind=kOutput, calls=%fused_computation.70 | convolution fusion | flops 1614807040 | bytes 16809984 | tf_op jit(solution)/shard_map/mjc,jnc->mnc/dot_general | solution.py:75
  1603.9 26.6 %fusion.54 = f32[64,512,1]{0,2,1:T(1,128)S(1)} fusion(f32[64,512,1]{0,2,1:T(1,128)S(1)} %bitcast.141, f32[512,64,64]{1,2,0:T(8,128)S(1)} %get-tuple-element.30, f32[64,512]{0,1:T(8,128)S(1)} %bitcast.138, f32[64,512]{0,1:T(8,128)S(1)} %get-tuple-element.22), kind=kOutput, calls=%fused_computation.89 | convolution fusion | flops 29360128 | bytes 8912896 | tf_op jit(solution)/shard_map/mkc,kc->mc/dot_general | solution.py:76
  1630.5 24.3 %fusion.12 = f32[512,64,64]{2,1,0:T(8,128)} fusion(f32[512,64,64]{2,1,0:T(8,128)} %fusion.26, f32[512,64,64]{2,1,0:T(8,128)} %fusion.27), kind=kOutput, calls=%fused_computation.45 | convolution fusion | flops 1610612736 | bytes 25165824 | tf_op jit(solution)/shard_map/mjc,jnc->mnc/dot_general | solution.py:73
  1654.7 21.8 %fusion.11 = f32[512,64,64]{2,1,0:T(8,128)S(1)} fusion(f32[512,64,64]{2,1,0:T(8,128)} %fusion.27, f32[512,64,64]{2,1,0:T(8,128)} %fusion.12, f32[64,64]{0,1:T(8,128)S(1)} %get-tuple-element.36), kind=kOutput, calls=%fused_computation.44 | convolution fusion | flops 1614807040 | bytes 25182208 | tf_op jit(solution)/shard_map/mjc,jnc->mnc/dot_general | solution.py:75
  1706.3 25.2 %bitcast_add_fusion = f32[64,128,512]{1,0,2:T(8,128)} fusion(f32[64,128,512]{1,0,2:T(8,128)} %copy.114, f32[512,64,64]{2,1,0:T(8,128)} %copy-done.2, f32[64,512]{0,1:T(8,128)S(1)} %divide_bitcast_fusion, f32[512]{0:T(512)S(1)} %get-tuple-element.23, f32[128,512]{0,1:T(8,128)S(1)} %copy.112), kind=kOutput, calls=%fused_computation.35 | convolution fusion | flops 3233808384 | bytes 42338304 | tf_op jit(solution)/shard_map/mvc,mnc->nvc/dot_general | solution.py:82
  1731.5 17.5 copy.123
  1749.0 24.6 %reshape.65 = f32[64,4,32,8,64]{4,3,2,1,0:T(8,128)} reshape(f32[64,128,512]{2,1,0:T(8,128)} %copy.123) | data formatting | bytes 33554432 | tf_op jit(solution)/shard_map/reshape | solution.py:111
  (96 shorter events, 188.2 us)
Async XLA Ops:
  0.0 170.6 %copy-start = (f32[4,4]{1,0:T(4,128)S(1)}, f32[4,4]{1,0:T(4,128)}, u32[]{:S(2)}) copy-start(f32[4,4]{1,0:T(4,128)} %param.9) | copy-start | bytes 196
  0.0 51.3 %slice-start = ((s8[16777216]{0:T(1024)(128)(4,1)}), s8[4194304]{0:T(1024)(128)(4,1)S(1)}, s32[]{:S(2)}) async-start(s8[16777216]{0:T(1024)(128)(4,1)} %bitcast.135), calls=%async_computation.1 | async-start | bytes 8388608
  0.0 51.3 %slice-start.1 = ((s8[16777216]{0:T(1024)(128)(4,1)}), s8[4194304]{0:T(1024)(128)(4,1)S(1)}, s32[]{:S(2)}) async-start(s8[16777216]{0:T(1024)(128)(4,1)} %bitcast.135), calls=%async_computation.2 | async-start | bytes 8388608
  0.0 51.3 %slice-start.2 = ((s8[16777216]{0:T(1024)(128)(4,1)}), s8[4194304]{0:T(1024)(128)(4,1)S(1)}, s32[]{:S(2)}) async-start(s8[16777216]{0:T(1024)(128)(4,1)} %bitcast.135), calls=%async_computation.3 | async-start | bytes 8388608
  19.3 43.8 %copy-start.3 = (f32[32,4,32,8,128]{4,1,3,2,0:T(4,128)}, f32[32,4,32,8,128]{4,1,3,2,0:T(4,128)S(1)}, u32[]{:S(2)}) copy-start(f32[32,4,32,8,128]{4,1,3,2,0:T(4,128)S(1)} %copy.101) | copy-start | bytes 50331652
  19.3 32.0 %slice-start.3 = ((s8[16777216]{0:T(1024)(128)(4,1)}), s8[4194304]{0:T(1024)(128)(4,1)S(1)}, s32[]{:S(2)}) async-start(s8[16777216]{0:T(1024)(128)(4,1)} %bitcast.135), calls=%async_computation.4 | async-start | bytes 8388608
  22.6 27.2 %collective-permute-start = (f32[32,4,32,1,128]{4,1,3,2,0:T(4,128)}, f32[32,4,32,1,128]{4,1,3,2,0:T(4,128)S(1)}, u32[]{:S(2)}, u32[]{:S(2)}) collective-permute-start(f32[32,4,32,1,128]{4,1,3,2,0:T(4,128)} %get-tuple-element.20), channel_id=1, source_target_pairs={{0,4},{4,8},{8,12},{1,5},{5,9},{9,13},{2,6},{6,10},{10,14},{3,7},{... | collective-permute-start | bytes 6291464 | tf_op jit(solution)/shard_map/ppermute | solution.py:17
  26.5 36.6 %collective-permute-start.1 = (f32[32,4,32,1,128]{4,1,3,2,0:T(4,128)}, f32[32,4,32,1,128]{4,1,3,2,0:T(4,128)S(1)}, u32[]{:S(2)}, u32[]{:S(2)}) collective-permute-start(f32[32,4,32,1,128]{4,1,3,2,0:T(4,128)} %get-tuple-element.19), channel_id=1, source_target_pairs={{4,0},{8,4},{12,8},{5,1},{9,5},{13,9},{6,2},{10,6},{14,10},{7,3},{... | collective-permute-start | bytes 6291464 | tf_op jit(solution)/shard_map/ppermute | solution.py:18
  49.8 13.3 copy-start.7
  63.1 1.3 copy-start.9
  94.8 43.3 %copy-start.13 = (f32[32]{0:T(128)S(1)}, f32[32]{0:T(128)}, u32[]{:S(2)}) copy-start(f32[32]{0:T(128)} %param.12) | copy-start | bytes 388
  94.8 43.3 %copy-start.14 = (f32[32]{0:T(128)S(1)}, f32[32]{0:T(128)}, u32[]{:S(2)}) copy-start(f32[32]{0:T(128)} %param.11) | copy-start | bytes 388
  112.7 25.4 %collective-permute-start.2 = (f32[32,4,32,10,1]{2,0,4,3,1:T(8,128)S(1)}, f32[32,4,32,10,1]{2,0,4,3,1:T(8,128)S(1)}, u32[]{:S(2)}, u32[]{:S(2)}) collective-permute-start(f32[32,4,32,10,1]{2,0,4,3,1:T(8,128)S(1)} %copy.90), channel_id=1, source_target_pairs={{0,1},{1,2},{2,3},{4,5},{5,6},{6,7},{8,9},{9,10},{10,11},{12,13},{... | collective-permute-start | bytes 491528 | tf_op jit(solution)/shard_map/ppermute | solution.py:17
  132.7 21.1 %collective-permute-start.3 = (f32[32,4,32,10,1]{2,0,4,3,1:T(8,128)}, f32[32,4,32,10,1]{2,0,4,3,1:T(8,128)}, u32[]{:S(2)}, u32[]{:S(2)}) collective-permute-start(f32[32,4,32,10,1]{2,0,4,3,1:T(8,128)} %copy.92), channel_id=1, source_target_pairs={{1,0},{2,1},{3,2},{5,4},{6,5},{7,6},{9,8},{10,9},{11,10},{13,12},{... | collective-permute-start | bytes 491528 | tf_op jit(solution)/shard_map/ppermute | solution.py:18
  138.1 32.5 %copy-start.8 = (f32[32,4,32,1,128]{4,1,3,2,0:T(4,128)S(1)}, f32[32,4,32,1,128]{4,1,3,2,0:T(4,128)}, u32[]{:S(2)}) copy-start(f32[32,4,32,1,128]{4,1,3,2,0:T(4,128)} %copy-done.7) | copy-start | bytes 6291460
  138.1 32.5 %copy-start.15 = (f32[32]{0:T(128)S(1)}, f32[32]{0:T(128)}, u32[]{:S(2)}) copy-start(f32[32]{0:T(128)} %param.10) | copy-start | bytes 388
  254.9 27.8 %collective-permute-start.4 = (f32[32,4,32,1,128]{4,1,3,2,0:T(4,128)S(1)}, f32[32,4,32,1,128]{4,1,3,2,0:T(4,128)S(1)}, u32[]{:S(2)}, u32[]{:S(2)}) collective-permute-start(f32[32,4,32,1,128]{4,1,3,2,0:T(4,128)S(1)} %get-tuple-element.17), channel_id=1, source_target_pairs={{0,4},{4,8},{8,12},{1,5},{5,9},{9,13},{2,6},{6,10},{10,14},{3,7},{... | collective-permute-start | bytes 6291464 | tf_op jit(solution)/shard_map/ppermute | solution.py:17
  259.8 27.4 %collective-permute-start.5 = (f32[32,4,32,1,128]{4,1,3,2,0:T(4,128)S(1)}, f32[32,4,32,1,128]{4,1,3,2,0:T(4,128)S(1)}, u32[]{:S(2)}, u32[]{:S(2)}) collective-permute-start(f32[32,4,32,1,128]{4,1,3,2,0:T(4,128)S(1)} %get-tuple-element.18), channel_id=1, source_target_pairs={{4,0},{8,4},{12,8},{5,1},{9,5},{13,9},{6,2},{10,6},{14,10},{7,3},{... | collective-permute-start | bytes 6291464 | tf_op jit(solution)/shard_map/ppermute | solution.py:18
  287.1 1.3 copy-start.5
  355.6 21.5 %collective-permute-start.7 = (f32[32,4,32,10,1]{2,0,4,3,1:T(8,128)S(1)}, f32[32,4,32,10,1]{2,0,4,3,1:T(8,128)S(1)}, u32[]{:S(2)}, u32[]{:S(2)}) collective-permute-start(f32[32,4,32,10,1]{2,0,4,3,1:T(8,128)S(1)} %copy.99), channel_id=1, source_target_pairs={{1,0},{2,1},{3,2},{5,4},{6,5},{7,6},{9,8},{10,9},{11,10},{13,12},{... | collective-permute-start | bytes 491528 | tf_op jit(solution)/shard_map/ppermute | solution.py:18
  375.7 16.2 collective-permute-start.6
  494.3 24.9 %collective-permute-start.8 = (f32[32,4,32,1,128]{4,1,3,2,0:T(4,128)S(1)}, f32[32,4,32,1,128]{4,1,3,2,0:T(4,128)S(1)}, u32[]{:S(2)}, u32[]{:S(2)}) collective-permute-start(f32[32,4,32,1,128]{4,1,3,2,0:T(4,128)S(1)} %get-tuple-element.15), channel_id=1, source_target_pairs={{0,4},{4,8},{8,12},{1,5},{5,9},{9,13},{2,6},{6,10},{10,14},{3,7},{... | collective-permute-start | bytes 6291464 | tf_op jit(solution)/shard_map/ppermute | solution.py:17
  496.3 27.4 %collective-permute-start.9 = (f32[32,4,32,1,128]{4,1,3,2,0:T(4,128)S(1)}, f32[32,4,32,1,128]{4,1,3,2,0:T(4,128)S(1)}, u32[]{:S(2)}, u32[]{:S(2)}) collective-permute-start(f32[32,4,32,1,128]{4,1,3,2,0:T(4,128)S(1)} %get-tuple-element.16), channel_id=1, source_target_pairs={{4,0},{8,4},{12,8},{5,1},{9,5},{13,9},{6,2},{10,6},{14,10},{7,3},{... | collective-permute-start | bytes 6291464 | tf_op jit(solution)/shard_map/ppermute | solution.py:18
  523.7 1.3 copy-start.6
  592.1 26.0 %collective-permute-start.10 = (f32[32,4,32,10,1]{2,0,4,3,1:T(8,128)S(1)}, f32[32,4,32,10,1]{2,0,4,3,1:T(8,128)S(1)}, u32[]{:S(2)}, u32[]{:S(2)}) collective-permute-start(f32[32,4,32,10,1]{2,0,4,3,1:T(8,128)S(1)} %copy.102), channel_id=1, source_target_pairs={{0,1},{1,2},{2,3},{4,5},{5,6},{6,7},{8,9},{9,10},{10,11},{12,13},{... | collective-permute-start | bytes 491528 | tf_op jit(solution)/shard_map/ppermute | solution.py:17
  612.1 21.6 %collective-permute-start.11 = (f32[32,4,32,10,1]{2,0,4,3,1:T(8,128)}, f32[32,4,32,10,1]{2,0,4,3,1:T(8,128)}, u32[]{:S(2)}, u32[]{:S(2)}) collective-permute-start(f32[32,4,32,10,1]{2,0,4,3,1:T(8,128)} %copy.104), channel_id=1, source_target_pairs={{1,0},{2,1},{3,2},{5,4},{6,5},{7,6},{9,8},{10,9},{11,10},{13,12},{... | collective-permute-start | bytes 491528 | tf_op jit(solution)/shard_map/ppermute | solution.py:18
  732.8 25.0 %collective-permute-start.12 = (f32[32,4,32,1,128]{4,1,3,2,0:T(4,128)S(1)}, f32[32,4,32,1,128]{4,1,3,2,0:T(4,128)S(1)}, u32[]{:S(2)}, u32[]{:S(2)}) collective-permute-start(f32[32,4,32,1,128]{4,1,3,2,0:T(4,128)S(1)} %get-tuple-element.13), channel_id=1, source_target_pairs={{0,4},{4,8},{8,12},{1,5},{5,9},{9,13},{2,6},{6,10},{10,14},{3,7},{... | collective-permute-start | bytes 6291464 | tf_op jit(solution)/shard_map/ppermute | solution.py:17
  734.8 27.4 %collective-permute-start.13 = (f32[32,4,32,1,128]{4,1,3,2,0:T(4,128)S(1)}, f32[32,4,32,1,128]{4,1,3,2,0:T(4,128)S(1)}, u32[]{:S(2)}, u32[]{:S(2)}) collective-permute-start(f32[32,4,32,1,128]{4,1,3,2,0:T(4,128)S(1)} %get-tuple-element.14), channel_id=1, source_target_pairs={{4,0},{8,4},{12,8},{5,1},{9,5},{13,9},{6,2},{10,6},{14,10},{7,3},{... | collective-permute-start | bytes 6291464 | tf_op jit(solution)/shard_map/ppermute | solution.py:18
  762.2 1.3 copy-start.4
  830.7 25.2 %collective-permute-start.14 = (f32[32,4,32,10,1]{2,0,4,3,1:T(8,128)S(1)}, f32[32,4,32,10,1]{2,0,4,3,1:T(8,128)S(1)}, u32[]{:S(2)}, u32[]{:S(2)}) collective-permute-start(f32[32,4,32,10,1]{2,0,4,3,1:T(8,128)S(1)} %copy.106), channel_id=1, source_target_pairs={{0,1},{1,2},{2,3},{4,5},{5,6},{6,7},{8,9},{9,10},{10,11},{12,13},{... | collective-permute-start | bytes 491528 | tf_op jit(solution)/shard_map/ppermute | solution.py:17
  850.7 20.9 %collective-permute-start.15 = (f32[32,4,32,10,1]{2,0,4,3,1:T(8,128)}, f32[32,4,32,10,1]{2,0,4,3,1:T(8,128)}, u32[]{:S(2)}, u32[]{:S(2)}) collective-permute-start(f32[32,4,32,10,1]{2,0,4,3,1:T(8,128)} %copy.108), channel_id=1, source_target_pairs={{1,0},{2,1},{3,2},{5,4},{6,5},{7,6},{9,8},{10,9},{11,10},{13,12},{... | collective-permute-start | bytes 491528 | tf_op jit(solution)/shard_map/ppermute | solution.py:18
  1076.0 9.9 copy-start.10
  1076.0 10.1 copy-start.11
  1076.0 10.2 copy-start.12
  1076.0 172.6 %all-to-all-start = ((f32[2,1,2097152]{2,1,0:T(1,128)}), f32[2,1,2097152]{2,1,0:T(1,128)}, u32[]{:S(2)}, u32[]{:S(2)}) async-start(f32[2,1,2097152]{2,1,0:T(1,128)} %reshape.73), calls=%async_computation | async-start | bytes 33554432 | tf_op jit(solution)/shard_map/all_to_all | solution.py:100
  1676.5 29.2 %copy-start.2 = (f32[512,64,64]{2,1,0:T(8,128)}, f32[512,64,64]{2,1,0:T(8,128)S(1)}, u32[]{:S(2)}) copy-start(f32[512,64,64]{2,1,0:T(8,128)S(1)} %fusion.11) | copy-start | bytes 25165828
  1731.5 42.1 %copy-start.1 = (f32[4,4]{1,0:T(4,128)S(1)}, f32[4,4]{1,0:T(4,128)}, u32[]{:S(2)}) copy-start(f32[4,4]{1,0:T(4,128)} %param.9) | copy-start | bytes 196
where the time goes:
time: 1790 us; the launch traced here: 1770 us
  local copies, waits for them, and re-layouts  758 us (42%)
  matrix products  567 us (32%)
  waiting for transfers between devices  259 us (14%)
  other arithmetic  134 us (7%)
  starting transfers between devices  54.6 us (3%)
    dot_general x4, matrix products, tendency(): jnp.einsum('vw,...wlij->...vlij', coupling, centre, precision=lax.Precisi...  322 us
    slice x11, local copies, waits for them, and re-layouts, extended(): last = lax.slice_in_dim(value, length - width, length, axis=dim)  196 us
    unnamed x45, local copies, waits for them, and re-layouts  164 us
    all_to_all x1, waiting for transfers between devices, body(): lax.all_to_all(state, 'mem', split_axis=4, concat_axis=0, tiled=True)  162 us
    ppermute x8, waiting for transfers between devices, extended(): before = lax.ppermute(last, axis, up)  83.4 us
    slice x5, local copies, waits for them, and re-layouts, extended(): first = lax.slice_in_dim(value, 0, width, axis=dim)  77.2 us
    ppermute x4, local copies, waits for them, and re-layouts, extended(): before = lax.ppermute(last, axis, up)  63.8 us
    ppermute x4, local copies, waits for them, and re-layouts, extended(): after = lax.ppermute(first, axis, down)  63.7 us
  transfers between devices with their start and end apart: 17, of which 8 were waited for; matrix products, arithmetic and copies ran while one was open for 8% of the time, Pallas kernels for 0%

commit v1 on v0

--- a/solution.py
+++ b/solution.py
@@ -1,10 +1,11 @@
 import jax
 import jax.numpy as jnp
 from jax import lax
+from jax.experimental import pallas as pl
+from jax.experimental.pallas import tpu as pltpu
 from jax.sharding import PartitionSpec as P
 
 STEPS = 2
-NS_ITERS = 2
 
 
 def extended(value, sides, width):
@@ -51,35 +52,90 @@
     return (state + 0.5 * (first + second), margin_width)
 
 
-def analyse(block, index, value, weight):
-    members = block.shape[0]
-    entries = block.shape[1]
-    highest = lax.Precision.HIGHEST
-    mean = jnp.mean(block, axis=0)
-    pert = block - mean[None]
-    onehot = (index[:, None, :] == jnp.arange(entries, dtype=jnp.int32)[None, :, None]).astype(
-        jnp.float32
-    )
-    measurement_data = jnp.einsum("mvc,kvc->mkc", block, onehot, precision=highest)
-    obs_mean = jnp.mean(measurement_data, axis=0)
-    obs_pert = measurement_data - obs_mean[None]
-    scaled = obs_pert * weight[None]
-    eye = jnp.eye(members, dtype=jnp.float32)[:, :, None]
-    system = jnp.einsum("mkc,nkc->mnc", scaled, obs_pert, precision=highest) + (members - 1.0) * eye
-    scale = jnp.sqrt(jnp.sum(system * system, axis=(0, 1)))
-    current = system / scale[None, None]
-    inverse = jnp.broadcast_to(eye, system.shape)
-    for sweep in range(NS_ITERS):
-        factor = 1.5 * eye - 0.5 * jnp.einsum("mjc,jnc->mnc", inverse, current, precision=highest)
-        current = jnp.einsum("mjc,jnc->mnc", current, factor, precision=highest)
-        inverse = jnp.einsum("mjc,jnc->mnc", factor, inverse, precision=highest)
-    gain_vec = jnp.einsum("mkc,kc->mc", scaled, value - obs_mean, precision=highest)
-    half_vec = jnp.einsum("mjc,jc->mc", inverse, gain_vec, precision=highest)
-    centre = jnp.einsum("mjc,jc->mc", inverse, half_vec, precision=highest) / scale[None]
-    analysis_coefficients = (
-        inverse * jnp.sqrt((members - 1.0) / scale)[None, None] + centre[:, None, :]
-    )
-    return mean[None] + jnp.einsum("mvc,mnc->nvc", pert, analysis_coefficients, precision=highest)
+def split(value):
+    high = value.astype(jnp.bfloat16)
+    return high, (value - high.astype(jnp.float32)).astype(jnp.bfloat16)
+
+
+def doubled(high, low, left):
+    both = jnp.where(left, high.astype(jnp.float32), low.astype(jnp.float32)).astype(jnp.bfloat16)
+    return jnp.concatenate([both, both], axis=1)
+
+
+def stacked(high, low):
+    return jnp.concatenate([high, high, low, low], axis=0)
+
+
+def product(left, right):
+    return lax.dot_general(left, right, (((1,), (0,)), ((), ())), preferred_element_type=jnp.float32)
+
+
+def product_t(left, right):
+    return lax.dot_general(left, right, (((1,), (1,)), ((), ())), preferred_element_type=jnp.float32)
+
+
+def analysis_kernel(x_ref, index_ref, root_ref, value_ref, out_ref):
+    count, members, entries = x_ref.shape
+    cells = range(count)
+    lane = lax.broadcasted_iota(jnp.int32, (members, 2 * members), 1)
+    row = lax.broadcasted_iota(jnp.int32, (members, 2 * members), 0)
+    left = lane < members
+    left_tall = lax.broadcasted_iota(jnp.int32, (members + 16, 2 * members), 1) < members
+    eye = jnp.where((lane == row) | (lane == row + members), 1.0, 0.0).astype(jnp.float32)
+    means, perts, systems, gains = [], [], [], []
+    for b in cells:
+        x = x_ref[b]
+        mean = jnp.sum(x, axis=0, keepdims=True) * (1.0 / members)
+        pert = x - mean
+        index = jnp.broadcast_to(index_ref[b : b + 1], (members, entries))
+        observed = jnp.take_along_axis(pert, index, axis=1)
+        obs_mean = jnp.take_along_axis(jnp.broadcast_to(mean, (8, entries)), index[:8], axis=1)
+        root = root_ref[b : b + 1]
+        innovation = (value_ref[b : b + 1] - obs_mean) * root
+        scaled = observed * root
+        high, low = split(jnp.concatenate([scaled, innovation, innovation], axis=0))
+        ahigh, alow = high[:members], low[:members]
+        wide = jnp.concatenate(
+            [jnp.concatenate([ahigh, alow], axis=1), jnp.concatenate([ahigh, alow], axis=1)], axis=0
+        )
+        both = product_t(doubled(high, low, left_tall), wide)
+        means.append(mean)
+        perts.append(pert)
+        systems.append(both[:members] + (members - 1.0) * eye)
+        gains.append(both[members : members + 1])
+    inverses, rates = [], []
+    for b in cells:
+        total = 0.5 * jnp.sum(jnp.sum(systems[b] * systems[b], axis=0, keepdims=True), axis=1, keepdims=True)
+        rates.append(lax.rsqrt(total))
+    for b in cells:
+        current = systems[b] * rates[b]
+        high, low = split(current)
+        square = product(doubled(high, low, left), stacked(high, low))
+        shigh, slow = split(square)
+        high, low = split(0.0625 * square - 0.5625 * current)
+        rest = product(doubled(shigh, slow, left), stacked(high, low))
+        inverses.append(2.25 * eye - 2.4375 * current + 1.6875 * square + rest)
+    for b in cells:
+        high, low = split(inverses[b])
+        phigh, plow = split(perts[b])
+        moved = product(doubled(high, low, left), stacked(phigh, plow))
+        half = 0.5 * jnp.sum(inverses[b] * gains[b], axis=1, keepdims=True)
+        shift = jnp.sum(moved * half, axis=0, keepdims=True) * rates[b]
+        out_ref[b] = moved * jnp.sqrt((members - 1.0) * rates[b]) + (means[b] + shift)
+
+
+def analyse(flat, index, value, weight):
+    cells, members, entries = flat.shape
+    count = 8
+    small = pl.BlockSpec((count, index.shape[1]), lambda i: (i, 0))
+    large = pl.BlockSpec((count, members, entries), lambda i: (i, 0, 0))
+    return pl.pallas_call(
+        analysis_kernel,
+        grid=(cells // count,),
+        in_specs=[large, small, small, small],
+        out_specs=large,
+        out_shape=jax.ShapeDtypeStruct(flat.shape, flat.dtype),
+    )(flat, index, jnp.sqrt(weight), value)
 
 
 def body(
@@ -100,14 +156,14 @@
     moved = lax.all_to_all(state, "mem", split_axis=4, concat_axis=0, tiled=True)
     members, variables, levels, rows_local, cols_local = moved.shape
     cells = rows_local * cols_local
-    flat = moved.reshape(members, variables * levels, cells)
-    observations = observed_entry_index.shape[0]
-    result = analyse(
-        flat,
-        observed_entry_index.reshape(observations, cells),
-        obs_value.reshape(observations, cells),
-        obs_weight.reshape(observations, cells),
-    )
+    flat = moved.reshape(members, variables * levels, cells).transpose(2, 0, 1)
+
+    def listed(array):
+        array = array.reshape(array.shape[0], cells).T
+        return jnp.concatenate([array, array], axis=1)
+
+    result = analyse(flat, listed(observed_entry_index), listed(obs_value), listed(obs_weight))
+    result = result.transpose(1, 2, 0)
     return result.reshape(members, variables, levels, rows_local, cols_local)
 
 

time: 1790 us -> 1600 us (0.89)
  matrix products: 567 us -> 320 us
  Pallas kernels: 0 us -> 65.9 us
    dot_general x11 -> x0, matrix products: 246 us -> none  [the longest x2 44.9 us: analyse(): jnp.einsum('mjc,jnc->mnc', inverse, current, precision=highest)]
    pallas_call x0 -> x1, Pallas kernels: none -> 65.9 us  [analyse(): pl.pallas_call(analysis_kernel, grid=(cells // count,), in_specs=[large,...]
    ppermute x8, waiting for transfers between devices: 83.4 us -> 24.9 us  [extended(): before = lax.ppermute(last, axis, up)]
    ppermute x8, waiting for transfers between devices: 13.2 us -> 65.3 us  [extended(): after = lax.ppermute(first, axis, down)]
    unnamed x45 -> x44, local copies, waits for them, and re-layouts: 164 us -> 164 us
    reshape x3 -> x2, local copies, waits for them, and re-layouts: 44.3 us -> 44.1 us  [body(): flat = moved.reshape(members, variables * levels, cells).transpose(2, 0, 1)]
  transfers between devices with their start and end apart: 17 -> 17, of which waited for: 8 -> 8; matrix products, arithmetic and copies ran while one was open for 8% -> 10% of each run, Pallas kernels for 0% -> 0%
where the time goes in v1:
time: 1600 us; the launch traced here: 1570 us
  local copies, waits for them, and re-layouts  757 us (47%)
  matrix products  320 us (20%)
  waiting for transfers between devices  249 us (16%)
  other arithmetic  124 us (8%)
  Pallas kernels  65.9 us (4%)
  starting transfers between devices  56.6 us (4%)
    dot_general x4, matrix products, tendency(): jnp.einsum('vw,...wlij->...vlij', coupling, centre, precision=lax.Precisi...  320 us
    slice x11, local copies, waits for them, and re-layouts, extended(): last = lax.slice_in_dim(value, length - width, length, axis=dim)  199 us
    unnamed x44, local copies, waits for them, and re-layouts  164 us
    all_to_all x1, waiting for transfers between devices, body(): lax.all_to_all(state, 'mem', split_axis=4, concat_axis=0, tiled=True)  159 us
    slice x5, local copies, waits for them, and re-layouts, extended(): first = lax.slice_in_dim(value, 0, width, axis=dim)  74.6 us
    ppermute x4, local copies, waits for them, and re-layouts, extended(): before = lax.ppermute(last, axis, up)  67.1 us
    pallas_call x1, Pallas kernels, analyse(): pl.pallas_call(analysis_kernel, grid=(cells // count,), in_specs=[large,...  65.9 us
    ppermute x8, waiting for transfers between devices, extended(): after = lax.ppermute(first, axis, down)  65.3 us
  transfers between devices with their start and end apart: 17, of which 8 were waited for; matrix products, arithmetic and copies ran while one was open for 10% of the time, Pallas kernels for 0%

profile of v1, /device:TPU:25, one launch (start us, length us, event | category | flops | bytes accessed | tf_op | source)
XLA Modules:
  0.0 1573.4 jit_solution(9779166877122441534)
XLA Ops:
  0.0 19.3 %copy.86 = f32[32,4,32,8,128]{4,1,3,2,0:T(4,128)S(1)} copy(f32[32,4,32,8,128]{4,3,2,1,0:T(8,128)} %param.8) | data formatting | bytes 33554432 | tf_op args[0]
  28.4 21.3 %collective-permute-done = f32[32,4,32,1,128]{4,1,3,2,0:T(4,128)S(1)} collective-permute-done((f32[32,4,32,1,128]{4,1,3,2,0:T(4,128)}, f32[32,4,32,1,128]{4,1,3,2,0:T(4,128)S(1)}, u32[]{:S(2)}, u32[]{:S(2)}) %collective-permute-start) | collective-permute-done | bytes 2097184 | tf_op jit(solution)/shard_map/ppermute | solution.py:18
  51.4 11.7 constant_dynamic-update-slice_fusion.1
  65.9 28.8 %fusion.13 = (f32[32,4,32,10,1]{4,1,3,2,0:T(4,128)}, f32[32,4,32,10,1]{4,1,3,2,0:T(4,128)}) fusion(f32[32,4,32,10,128]{4,1,3,2,0:T(4,128)} %constant_dynamic-update-slice_fusion), kind=kLoop, calls=%fused_computation.57 | loop fusion | bytes 655360 | tf_op jit(solution)/shard_map/slice | solution.py:16
  94.8 17.8 %copy.77 = f32[32,4,32,10,1]{2,0,4,3,1:T(8,128)S(1)} copy(f32[32,4,32,10,1]{4,1,3,2,0:T(4,128)} %get-tuple-element.12) | data formatting | bytes 327680 | tf_op jit(solution)/shard_map/slice | solution.py:17
  114.7 18.7 %copy.75 = f32[32,4,32,10,1]{2,0,4,3,1:T(8,128)} copy(f32[32,4,32,10,1]{4,1,3,2,0:T(4,128)} %get-tuple-element.11) | data formatting | bytes 327680 | tf_op jit(solution)/shard_map/slice | solution.py:16
  135.0 15.6 copy.78
  150.6 16.8 %copy.76 = f32[32,4,32,10,1]{4,1,3,2,0:T(4,128)} copy(f32[32,4,32,10,1]{2,0,4,3,1:T(8,128)} %collective-permute-done.2) | data formatting | bytes 327680 | tf_op jit(solution)/shard_map/ppermute | solution.py:18
  167.4 81.5 %copy_add_fusion = (f32[32,4,32,8,128]{4,1,3,2,0:T(4,128)}, f32[32,4,32,8,128]{4,1,3,2,0:T(4,128)}) fusion(f32[32,4,32,8,128]{4,3,2,1,0:T(8,128)} %param.8, f32[32,4,32,8,128]{4,1,3,2,0:T(4,128)} %copy-done.1, f32[4,4]{1,0:T(4,128)S(1)} %copy-done, f32[32]{0:T(128)S(1)} %get-tuple-element.25, f32[32]{0:T(128)S(1)} %get-tuple-element.26, ...), kind=kOutput, calls=%fused_computation.53 | convolution fusion | flops 276824064 | bytes 92602816 | tf_op jit(solution)/shard_map/vw,...wlij->...vlij/dot_general | solution.py:31
  253.5 4.6 collective-permute-start.4
  258.1 21.8 %collective-permute-done.5 = f32[32,4,32,1,128]{4,1,3,2,0:T(4,128)S(1)} collective-permute-done((f32[32,4,32,1,128]{4,1,3,2,0:T(4,128)S(1)}, f32[32,4,32,1,128]{4,1,3,2,0:T(4,128)S(1)}, u32[]{:S(2)}, u32[]{:S(2)}) %collective-permute-start.5) | collective-permute-done | bytes 2097184 | tf_op jit(solution)/shard_map/ppermute | solution.py:19
  282.4 20.4 %pad_maximum_fusion = f32[32,4,32,10,128]{4,1,3,2,0:T(4,128)} fusion(f32[32,4,32,1,128]{4,1,3,2,0:T(4,128)S(1)} %collective-permute-done.5, f32[32,4,32,8,128]{4,1,3,2,0:T(4,128)} %get-tuple-element.21, f32[32,4,32,1,128]{4,1,3,2,0:T(4,128)S(1)} %collective-permute-done.4), kind=kLoop, calls=%fused_computation | loop fusion | flops 10485760 | bytes 41943040 | tf_op jit(solution)/shard_map/concatenate | solution.py:20
  302.8 28.9 %fusion.12 = (f32[32,4,32,10,1]{4,1,3,2,0:T(4,128)}, f32[32,4,32,10,1]{4,1,3,2,0:T(4,128)}) fusion(f32[32,4,32,10,128]{4,1,3,2,0:T(4,128)} %pad_maximum_fusion), kind=kLoop, calls=%fused_computation.56 | loop fusion | bytes 655360 | tf_op jit(solution)/shard_map/slice | solution.py:16
  331.7 17.8 %copy.84 = f32[32,4,32,10,1]{2,0,4,3,1:T(8,128)S(1)} copy(f32[32,4,32,10,1]{4,1,3,2,0:T(4,128)} %get-tuple-element.10) | data formatting | bytes 327680 | tf_op jit(solution)/shard_map/slice | solution.py:17
  353.9 18.7 %copy.82 = f32[32,4,32,10,1]{2,0,4,3,1:T(8,128)} copy(f32[32,4,32,10,1]{4,1,3,2,0:T(4,128)} %get-tuple-element.9) | data formatting | bytes 327680 | tf_op jit(solution)/shard_map/slice | solution.py:16
  374.3 14.7 copy.85
  389.0 16.8 %copy.83 = f32[32,4,32,10,1]{4,1,3,2,0:T(4,128)} copy(f32[32,4,32,10,1]{2,0,4,3,1:T(8,128)} %collective-permute-done.6) | data formatting | bytes 327680 | tf_op jit(solution)/shard_map/ppermute | solution.py:18
  405.7 82.9 %fusion.5 = f32[32,4,32,8,128]{4,1,3,2,0:T(4,128)} fusion(f32[32,4,32,8,128]{4,1,3,2,0:T(4,128)} %get-tuple-element.22, f32[32,4,32,8,128]{4,1,3,2,0:T(4,128)} %get-tuple-element.21, f32[32,4,32,10,1]{4,1,3,2,0:T(4,128)} %copy.85, f32[32,4,32,1,128]{4,1,3,2,0:T(4,128)S(1)} %collective-permute-done.5, f32[32,4,32,1,128]{4,1,3,2,0:T(4,128)} %copy-done.3, ...), kind=kOutput, calls=%fused_computation.39 | convolution fusion | flops 301989888 | bytes 71631296 | tf_op jit(solution)/shard_map/vw,...wlij->...vlij/dot_general | solution.py:31
  493.3 4.7 collective-permute-start.8
  498.0 21.8 %collective-permute-done.9 = f32[32,4,32,1,128]{4,1,3,2,0:T(4,128)S(1)} collective-permute-done((f32[32,4,32,1,128]{4,1,3,2,0:T(4,128)S(1)}, f32[32,4,32,1,128]{4,1,3,2,0:T(4,128)S(1)}, u32[]{:S(2)}, u32[]{:S(2)}) %collective-permute-start.9) | collective-permute-done | bytes 2097184 | tf_op jit(solution)/shard_map/ppermute | solution.py:19
  522.3 20.4 %pad_maximum_fusion.1 = f32[32,4,32,10,128]{4,1,3,2,0:T(4,128)} fusion(f32[32,4,32,1,128]{4,1,3,2,0:T(4,128)S(1)} %collective-permute-done.9, f32[32,4,32,8,128]{4,1,3,2,0:T(4,128)} %fusion.5, f32[32,4,32,1,128]{4,1,3,2,0:T(4,128)S(1)} %collective-permute-done.8), kind=kLoop, calls=%fused_computation.1 | loop fusion | flops 10485760 | bytes 41943040 | tf_op jit(solution)/shard_map/concatenate | solution.py:20
  542.7 28.9 %fusion.11 = (f32[32,4,32,10,1]{4,1,3,2,0:T(4,128)}, f32[32,4,32,10,1]{4,1,3,2,0:T(4,128)}) fusion(f32[32,4,32,10,128]{4,1,3,2,0:T(4,128)} %pad_maximum_fusion.1), kind=kLoop, calls=%fused_computation.55 | loop fusion | bytes 655360 | tf_op jit(solution)/shard_map/slice | solution.py:16
  571.5 17.8 %copy.89 = f32[32,4,32,10,1]{2,0,4,3,1:T(8,128)S(1)} copy(f32[32,4,32,10,1]{4,1,3,2,0:T(4,128)} %get-tuple-element.8) | data formatting | bytes 327680 | tf_op jit(solution)/shard_map/slice | solution.py:17
  593.7 18.7 %copy.87 = f32[32,4,32,10,1]{2,0,4,3,1:T(8,128)} copy(f32[32,4,32,10,1]{4,1,3,2,0:T(4,128)} %get-tuple-element.7) | data formatting | bytes 327680 | tf_op jit(solution)/shard_map/slice | solution.py:16
  613.8 14.7 copy.90
  628.6 16.8 %copy.88 = f32[32,4,32,10,1]{4,1,3,2,0:T(4,128)} copy(f32[32,4,32,10,1]{2,0,4,3,1:T(8,128)} %collective-permute-done.10) | data formatting | bytes 327680 | tf_op jit(solution)/shard_map/ppermute | solution.py:18
  645.3 78.9 %fusion.18 = (f32[32,4,32,8,128]{4,1,3,2,0:T(4,128)}, f32[32,4,32,8,128]{4,1,3,2,0:T(4,128)}) fusion(f32[32,4,32,8,128]{4,1,3,2,0:T(4,128)} %fusion.5, f32[4,4]{1,0:T(4,128)S(1)} %copy-done, f32[32]{0:T(128)S(1)} %get-tuple-element.25, f32[32]{0:T(128)S(1)} %get-tuple-element.26, f32[32,4,32,10,1]{4,1,3,2,0:T(4,128)} %copy.90, ...), kind=kOutput, calls=%fused_computation.62 | convolution fusion | flops 293601280 | bytes 54854080 | tf_op jit(solution)/shard_map/vw,...wlij->...vlij/dot_general | solution.py:31
  728.9 4.7 collective-permute-start.12
  733.6 21.8 %collective-permute-done.13 = f32[32,4,32,1,128]{4,1,3,2,0:T(4,128)S(1)} collective-permute-done((f32[32,4,32,1,128]{4,1,3,2,0:T(4,128)S(1)}, f32[32,4,32,1,128]{4,1,3,2,0:T(4,128)S(1)}, u32[]{:S(2)}, u32[]{:S(2)}) %collective-permute-start.13) | collective-permute-done | bytes 2097184 | tf_op jit(solution)/shard_map/ppermute | solution.py:19
  757.8 20.4 %pad_maximum_fusion.2 = f32[32,4,32,10,128]{4,1,3,2,0:T(4,128)} fusion(f32[32,4,32,1,128]{4,1,3,2,0:T(4,128)S(1)} %collective-permute-done.13, f32[32,4,32,8,128]{4,1,3,2,0:T(4,128)} %get-tuple-element.23, f32[32,4,32,1,128]{4,1,3,2,0:T(4,128)S(1)} %collective-permute-done.12), kind=kLoop, calls=%fused_computation.2 | loop fusion | flops 10485760 | bytes 41943040 | tf_op jit(solution)/shard_map/concatenate | solution.py:20
  778.2 28.9 %fusion.10 = (f32[32,4,32,10,1]{4,1,3,2,0:T(4,128)}, f32[32,4,32,10,1]{4,1,3,2,0:T(4,128)}) fusion(f32[32,4,32,10,128]{4,1,3,2,0:T(4,128)} %pad_maximum_fusion.2), kind=kLoop, calls=%fused_computation.54 | loop fusion | bytes 655360 | tf_op jit(solution)/shard_map/slice | solution.py:16
  807.2 17.8 %copy.93 = f32[32,4,32,10,1]{2,0,4,3,1:T(8,128)S(1)} copy(f32[32,4,32,10,1]{4,1,3,2,0:T(4,128)} %get-tuple-element.6) | data formatting | bytes 327680 | tf_op jit(solution)/shard_map/slice | solution.py:17
  829.3 18.7 %copy.91 = f32[32,4,32,10,1]{2,0,4,3,1:T(8,128)} copy(f32[32,4,32,10,1]{4,1,3,2,0:T(4,128)} %get-tuple-element.5) | data formatting | bytes 327680 | tf_op jit(solution)/shard_map/slice | solution.py:16
  849.5 14.7 copy.94
  864.3 16.8 %copy.92 = f32[32,4,32,10,1]{4,1,3,2,0:T(4,128)} copy(f32[32,4,32,10,1]{2,0,4,3,1:T(8,128)} %collective-permute-done.14) | data formatting | bytes 327680 | tf_op jit(solution)/shard_map/ppermute | solution.py:18
  881.0 76.8 %fusion.2 = f32[32,4,32,8,128]{4,1,3,2,0:T(4,128)} fusion(f32[32,4,32,8,128]{4,1,3,2,0:T(4,128)} %fusion.5, f32[32,4,32,8,128]{4,1,3,2,0:T(4,128)} %get-tuple-element.24, f32[32,4,32,8,128]{4,1,3,2,0:T(4,128)} %get-tuple-element.23, f32[32,4,32,10,1]{4,1,3,2,0:T(4,128)} %copy.94, f32[32,4,32,1,128]{4,1,3,2,0:T(4,128)S(1)} %collective-permute-done.13, ...), kind=kOutput, calls=%fused_computation.34 | convolution fusion | flops 301989888 | bytes 71631296 | tf_op jit(solution)/shard_map/vw,...wlij->...vlij/dot_general | solution.py:31
  957.8 50.7 %copy.95 = f32[32,4,32,8,128]{2,3,1,0,4:T(8,128)} copy(f32[32,4,32,8,128]{4,1,3,2,0:T(4,128)} %fusion.2) | data formatting | bytes 33554432 | tf_op jit(solution)/shard_map/add | solution.py:52
  1008.5 61.1 %reshape.29 = f32[2,1,2097152]{2,1,0:T(1,128)} reshape(f32[128,32,4,8,32]{4,3,2,1,0:T(8,128)} %bitcast.46) | data formatting | bytes 33554432
  1069.6 9.9 all-to-all-start
  1081.9 159.2 %all-to-all-done = f32[2,1,2097152]{2,1,0:T(1,128)} async-done(((f32[2,1,2097152]{2,1,0:T(1,128)}), f32[2,1,2097152]{2,1,0:T(1,128)}, u32[]{:S(2)}, u32[]{:S(2)}) %all-to-all-start) | async-done | bytes 16777248 | tf_op jit(solution)/shard_map/all_to_all | solution.py:156
  1241.6 60.7 %reduce = f32[2,2097152]{1,0:T(2,128)} reduce(f32[2,1,2097152]{2,1,0:T(1,128)} %all-to-all-done, f32[]{:T(128)} %broadcast.25), dimensions={1}, to_apply=%all_to_all.11.reduce_sub_computation | reduce | bytes 33554436 | tf_op jit(solution)/shard_map/all_to_all | solution.py:156
  1302.3 64.7 %reshape.30 = f32[128,32,4,8,32]{4,3,2,1,0:T(8,128)} reshape(f32[2,2097152]{1,0:T(2,128)} %reduce) | data formatting | bytes 33554432
  1367.1 53.7 %copy.96 = f32[32,4,32,8,2,64]{5,3,2,1,0,4:T(8,128)} copy(f32[32,4,32,8,2,64]{2,3,1,0,5,4:T(8,128)} %bitcast.7) | data formatting | bytes 33554432 | tf_op jit(solution)/shard_map/all_to_all | solution.py:156
  1420.8 27.6 %reshape.23 = f32[64,128,512]{2,1,0:T(8,128)} reshape(f32[2,32,4,32,8,64]{5,4,3,2,1,0:T(8,128)} %bitcast.56) | data formatting | bytes 33554432 | tf_op jit(solution)/shard_map/reshape | solution.py:159
  1448.4 16.5 %copy.97 = f32[64,128,512]{1,0,2:T(8,128)} copy(f32[64,128,512]{2,1,0:T(8,128)} %reshape.23) | data formatting | bytes 33554432 | tf_op jit(solution)/shard_map/reshape | solution.py:159
  1464.9 65.9 %shard_map.82 = f32[512,64,128]{2,1,0:T(8,128)} custom-call(f32[512,64,128]{2,1,0:T(8,128)} %bitcast.59, s32[512,128]{1,0:T(8,128)} %pad_add_fusion.index_ref, f32[512,128]{1,0:T(8,128)} %get-tuple-element.27.root_ref, f32[512,128]{1,0:T(8,128)} %get-tuple-element.28.value_ref), custom_call_target="tpu_custom_call" | custom-call | tf_op jit(solution)/shard_map/pallas_call | solution.py:132
  1530.8 17.5 %copy.101 = f32[64,128,512]{2,1,0:T(8,128)} copy(f32[64,128,512]{1,0,2:T(8,128)} %bitcast.60) | data formatting | bytes 33554432 | tf_op jit(solution)/shard_map/transpose | solution.py:166
  1548.4 24.6 %reshape.27 = f32[64,4,32,8,64]{4,3,2,1,0:T(8,128)} reshape(f32[64,128,512]{2,1,0:T(8,128)} %copy.101) | data formatting | bytes 33554432 | tf_op jit(solution)/shard_map/reshape | solution.py:167
  (75 shorter events, 58.9 us)
Async XLA Ops:
  0.0 167.4 %copy-start = (f32[4,4]{1,0:T(4,128)S(1)}, f32[4,4]{1,0:T(4,128)}, u32[]{:S(2)}) copy-start(f32[4,4]{1,0:T(4,128)} %param.9) | copy-start | bytes 196
  0.0 51.3 %slice-start = ((s8[16777216]{0:T(1024)(128)(4,1)}), s8[4194304]{0:T(1024)(128)(4,1)S(1)}, s32[]{:S(2)}) async-start(s8[16777216]{0:T(1024)(128)(4,1)} %bitcast.57), calls=%async_computation.1 | async-start | bytes 8388608
  0.0 51.3 %slice-start.1 = ((s8[16777216]{0:T(1024)(128)(4,1)}), s8[4194304]{0:T(1024)(128)(4,1)S(1)}, s32[]{:S(2)}) async-start(s8[16777216]{0:T(1024)(128)(4,1)} %bitcast.57), calls=%async_computation.2 | async-start | bytes 8388608
  0.0 51.3 %slice-start.2 = ((s8[16777216]{0:T(1024)(128)(4,1)}), s8[4194304]{0:T(1024)(128)(4,1)S(1)}, s32[]{:S(2)}) async-start(s8[16777216]{0:T(1024)(128)(4,1)} %bitcast.57), calls=%async_computation.3 | async-start | bytes 8388608
  19.3 43.8 %copy-start.1 = (f32[32,4,32,8,128]{4,1,3,2,0:T(4,128)}, f32[32,4,32,8,128]{4,1,3,2,0:T(4,128)S(1)}, u32[]{:S(2)}) copy-start(f32[32,4,32,8,128]{4,1,3,2,0:T(4,128)S(1)} %copy.86) | copy-start | bytes 50331652
  19.3 32.0 %slice-start.3 = ((s8[16777216]{0:T(1024)(128)(4,1)}), s8[4194304]{0:T(1024)(128)(4,1)S(1)}, s32[]{:S(2)}) async-start(s8[16777216]{0:T(1024)(128)(4,1)} %bitcast.57), calls=%async_computation.4 | async-start | bytes 8388608
  22.6 27.2 %collective-permute-start = (f32[32,4,32,1,128]{4,1,3,2,0:T(4,128)}, f32[32,4,32,1,128]{4,1,3,2,0:T(4,128)S(1)}, u32[]{:S(2)}, u32[]{:S(2)}) collective-permute-start(f32[32,4,32,1,128]{4,1,3,2,0:T(4,128)} %get-tuple-element.20), channel_id=1, source_target_pairs={{0,4},{4,8},{8,12},{1,5},{5,9},{9,13},{2,6},{6,10},{10,14},{3,7},{... | collective-permute-start | bytes 6291464 | tf_op jit(solution)/shard_map/ppermute | solution.py:18
  26.5 36.6 %collective-permute-start.1 = (f32[32,4,32,1,128]{4,1,3,2,0:T(4,128)}, f32[32,4,32,1,128]{4,1,3,2,0:T(4,128)S(1)}, u32[]{:S(2)}, u32[]{:S(2)}) collective-permute-start(f32[32,4,32,1,128]{4,1,3,2,0:T(4,128)} %get-tuple-element.19), channel_id=1, source_target_pairs={{4,0},{8,4},{12,8},{5,1},{9,5},{13,9},{6,2},{10,6},{14,10},{7,3},{... | collective-permute-start | bytes 6291464 | tf_op jit(solution)/shard_map/ppermute | solution.py:19
  49.8 13.3 copy-start.5
  63.1 1.3 copy-start.7
  94.7 40.2 %copy-start.11 = (f32[32]{0:T(128)S(1)}, f32[32]{0:T(128)}, u32[]{:S(2)}) copy-start(f32[32]{0:T(128)} %param.12) | copy-start | bytes 388
  94.7 40.2 %copy-start.12 = (f32[32]{0:T(128)S(1)}, f32[32]{0:T(128)}, u32[]{:S(2)}) copy-start(f32[32]{0:T(128)} %param.11) | copy-start | bytes 388
  112.6 22.4 %collective-permute-start.3 = (f32[32,4,32,10,1]{2,0,4,3,1:T(8,128)S(1)}, f32[32,4,32,10,1]{2,0,4,3,1:T(8,128)S(1)}, u32[]{:S(2)}, u32[]{:S(2)}) collective-permute-start(f32[32,4,32,10,1]{2,0,4,3,1:T(8,128)S(1)} %copy.77), channel_id=1, source_target_pairs={{1,0},{2,1},{3,2},{5,4},{6,5},{7,6},{9,8},{10,9},{11,10},{13,12},{... | collective-permute-start | bytes 491528 | tf_op jit(solution)/shard_map/ppermute | solution.py:19
  133.4 17.2 %collective-permute-start.2 = (f32[32,4,32,10,1]{2,0,4,3,1:T(8,128)}, f32[32,4,32,10,1]{2,0,4,3,1:T(8,128)}, u32[]{:S(2)}, u32[]{:S(2)}) collective-permute-start(f32[32,4,32,10,1]{2,0,4,3,1:T(8,128)} %copy.75), channel_id=1, source_target_pairs={{0,1},{1,2},{2,3},{4,5},{5,6},{6,7},{8,9},{9,10},{10,11},{12,13},{... | collective-permute-start | bytes 491528 | tf_op jit(solution)/shard_map/ppermute | solution.py:18
  134.9 32.4 %copy-start.6 = (f32[32,4,32,1,128]{4,1,3,2,0:T(4,128)S(1)}, f32[32,4,32,1,128]{4,1,3,2,0:T(4,128)}, u32[]{:S(2)}) copy-start(f32[32,4,32,1,128]{4,1,3,2,0:T(4,128)} %copy-done.5) | copy-start | bytes 6291460
  134.9 32.4 %copy-start.13 = (f32[32]{0:T(128)S(1)}, f32[32]{0:T(128)}, u32[]{:S(2)}) copy-start(f32[32]{0:T(128)} %param.10) | copy-start | bytes 388
  251.6 28.3 %collective-permute-start.5 = (f32[32,4,32,1,128]{4,1,3,2,0:T(4,128)S(1)}, f32[32,4,32,1,128]{4,1,3,2,0:T(4,128)S(1)}, u32[]{:S(2)}, u32[]{:S(2)}) collective-permute-start(f32[32,4,32,1,128]{4,1,3,2,0:T(4,128)S(1)} %get-tuple-element.18), channel_id=1, source_target_pairs={{4,0},{8,4},{12,8},{5,1},{9,5},{13,9},{6,2},{10,6},{14,10},{7,3},{... | collective-permute-start | bytes 6291464 | tf_op jit(solution)/shard_map/ppermute | solution.py:19
  253.5 27.5 %collective-permute-start.4 = (f32[32,4,32,1,128]{4,1,3,2,0:T(4,128)S(1)}, f32[32,4,32,1,128]{4,1,3,2,0:T(4,128)S(1)}, u32[]{:S(2)}, u32[]{:S(2)}) collective-permute-start(f32[32,4,32,1,128]{4,1,3,2,0:T(4,128)S(1)} %get-tuple-element.17), channel_id=1, source_target_pairs={{0,4},{4,8},{8,12},{1,5},{5,9},{9,13},{2,6},{6,10},{10,14},{3,7},{... | collective-permute-start | bytes 6291464 | tf_op jit(solution)/shard_map/ppermute | solution.py:18
  281.1 1.3 copy-start.3
  349.5 24.7 %collective-permute-start.7 = (f32[32,4,32,10,1]{2,0,4,3,1:T(8,128)S(1)}, f32[32,4,32,10,1]{2,0,4,3,1:T(8,128)S(1)}, u32[]{:S(2)}, u32[]{:S(2)}) collective-permute-start(f32[32,4,32,10,1]{2,0,4,3,1:T(8,128)S(1)} %copy.84), channel_id=1, source_target_pairs={{1,0},{2,1},{3,2},{5,4},{6,5},{7,6},{9,8},{10,9},{11,10},{13,12},{... | collective-permute-start | bytes 491528 | tf_op jit(solution)/shard_map/ppermute | solution.py:19
  372.5 16.4 %collective-permute-start.6 = (f32[32,4,32,10,1]{2,0,4,3,1:T(8,128)}, f32[32,4,32,10,1]{2,0,4,3,1:T(8,128)}, u32[]{:S(2)}, u32[]{:S(2)}) collective-permute-start(f32[32,4,32,10,1]{2,0,4,3,1:T(8,128)} %copy.82), channel_id=1, source_target_pairs={{0,1},{1,2},{2,3},{4,5},{5,6},{6,7},{8,9},{9,10},{10,11},{12,13},{... | collective-permute-start | bytes 491528 | tf_op jit(solution)/shard_map/ppermute | solution.py:18
  491.4 28.4 %collective-permute-start.9 = (f32[32,4,32,1,128]{4,1,3,2,0:T(4,128)S(1)}, f32[32,4,32,1,128]{4,1,3,2,0:T(4,128)S(1)}, u32[]{:S(2)}, u32[]{:S(2)}) collective-permute-start(f32[32,4,32,1,128]{4,1,3,2,0:T(4,128)S(1)} %get-tuple-element.16), channel_id=1, source_target_pairs={{4,0},{8,4},{12,8},{5,1},{9,5},{13,9},{6,2},{10,6},{14,10},{7,3},{... | collective-permute-start | bytes 6291464 | tf_op jit(solution)/shard_map/ppermute | solution.py:19
  493.3 27.6 %collective-permute-start.8 = (f32[32,4,32,1,128]{4,1,3,2,0:T(4,128)S(1)}, f32[32,4,32,1,128]{4,1,3,2,0:T(4,128)S(1)}, u32[]{:S(2)}, u32[]{:S(2)}) collective-permute-start(f32[32,4,32,1,128]{4,1,3,2,0:T(4,128)S(1)} %get-tuple-element.15), channel_id=1, source_target_pairs={{0,4},{4,8},{8,12},{1,5},{5,9},{9,13},{2,6},{6,10},{10,14},{3,7},{... | collective-permute-start | bytes 6291464 | tf_op jit(solution)/shard_map/ppermute | solution.py:18
  521.0 1.3 copy-start.4
  589.4 24.5 %collective-permute-start.11 = (f32[32,4,32,10,1]{2,0,4,3,1:T(8,128)S(1)}, f32[32,4,32,10,1]{2,0,4,3,1:T(8,128)S(1)}, u32[]{:S(2)}, u32[]{:S(2)}) collective-permute-start(f32[32,4,32,10,1]{2,0,4,3,1:T(8,128)S(1)} %copy.89), channel_id=1, source_target_pairs={{1,0},{2,1},{3,2},{5,4},{6,5},{7,6},{9,8},{10,9},{11,10},{13,12},{... | collective-permute-start | bytes 491528 | tf_op jit(solution)/shard_map/ppermute | solution.py:19
  612.4 16.2 %collective-permute-start.10 = (f32[32,4,32,10,1]{2,0,4,3,1:T(8,128)}, f32[32,4,32,10,1]{2,0,4,3,1:T(8,128)}, u32[]{:S(2)}, u32[]{:S(2)}) collective-permute-start(f32[32,4,32,10,1]{2,0,4,3,1:T(8,128)} %copy.87), channel_id=1, source_target_pairs={{0,1},{1,2},{2,3},{4,5},{5,6},{6,7},{8,9},{9,10},{10,11},{12,13},{... | collective-permute-start | bytes 491528 | tf_op jit(solution)/shard_map/ppermute | solution.py:18
  727.0 28.4 %collective-permute-start.13 = (f32[32,4,32,1,128]{4,1,3,2,0:T(4,128)S(1)}, f32[32,4,32,1,128]{4,1,3,2,0:T(4,128)S(1)}, u32[]{:S(2)}, u32[]{:S(2)}) collective-permute-start(f32[32,4,32,1,128]{4,1,3,2,0:T(4,128)S(1)} %get-tuple-element.14), channel_id=1, source_target_pairs={{4,0},{8,4},{12,8},{5,1},{9,5},{13,9},{6,2},{10,6},{14,10},{7,3},{... | collective-permute-start | bytes 6291464 | tf_op jit(solution)/shard_map/ppermute | solution.py:19
  728.9 27.6 %collective-permute-start.12 = (f32[32,4,32,1,128]{4,1,3,2,0:T(4,128)S(1)}, f32[32,4,32,1,128]{4,1,3,2,0:T(4,128)S(1)}, u32[]{:S(2)}, u32[]{:S(2)}) collective-permute-start(f32[32,4,32,1,128]{4,1,3,2,0:T(4,128)S(1)} %get-tuple-element.13), channel_id=1, source_target_pairs={{0,4},{4,8},{8,12},{1,5},{5,9},{9,13},{2,6},{6,10},{10,14},{3,7},{... | collective-permute-start | bytes 6291464 | tf_op jit(solution)/shard_map/ppermute | solution.py:18
  756.5 1.3 copy-start.2
  825.0 24.5 %collective-permute-start.15 = (f32[32,4,32,10,1]{2,0,4,3,1:T(8,128)S(1)}, f32[32,4,32,10,1]{2,0,4,3,1:T(8,128)S(1)}, u32[]{:S(2)}, u32[]{:S(2)}) collective-permute-start(f32[32,4,32,10,1]{2,0,4,3,1:T(8,128)S(1)} %copy.93), channel_id=1, source_target_pairs={{1,0},{2,1},{3,2},{5,4},{6,5},{7,6},{9,8},{10,9},{11,10},{13,12},{... | collective-permute-start | bytes 491528 | tf_op jit(solution)/shard_map/ppermute | solution.py:19
  848.0 16.2 %collective-permute-start.14 = (f32[32,4,32,10,1]{2,0,4,3,1:T(8,128)}, f32[32,4,32,10,1]{2,0,4,3,1:T(8,128)}, u32[]{:S(2)}, u32[]{:S(2)}) collective-permute-start(f32[32,4,32,10,1]{2,0,4,3,1:T(8,128)} %copy.91), channel_id=1, source_target_pairs={{0,1},{1,2},{2,3},{4,5},{5,6},{6,7},{8,9},{9,10},{10,11},{12,13},{... | collective-permute-start | bytes 491528 | tf_op jit(solution)/shard_map/ppermute | solution.py:18
  1069.6 10.0 copy-start.8
  1069.6 10.1 copy-start.9
  1069.6 10.3 copy-start.10
  1069.6 171.4 %all-to-all-start = ((f32[2,1,2097152]{2,1,0:T(1,128)}), f32[2,1,2097152]{2,1,0:T(1,128)}, u32[]{:S(2)}, u32[]{:S(2)}) async-start(f32[2,1,2097152]{2,1,0:T(1,128)} %reshape.29), calls=%async_computation | async-start | bytes 33554432 | tf_op jit(solution)/shard_map/all_to_all | solution.py:156

commit v2 on v1

v2 whole, which is shorter than its diff:
```python
import jax
import jax.numpy as jnp
from jax import lax
from jax.experimental import pallas as pl
from jax.experimental.pallas import tpu as pltpu
from jax.sharding import PartitionSpec as P

STEPS = 2
PARTS = 2


def pack(value, place, lane, sides):
    west, east = sides
    here = lane == place
    return (
        jnp.where(here, pltpu.roll(value, place, 1), west),
        jnp.where(here, pltpu.roll(value, place + 1, 1), east),
    )


def borders_kernel(x_ref, north_ref, south_ref, west_ref, east_ref):
    _, variables, levels, rows, cols = x_ref.shape
    lane = lax.broadcasted_iota(jnp.int32, (rows, cols), 1)

    def level(l, sides):
        for v in range(variables):
            value, place = x_ref[0, v, l], v * levels + l
            north_ref[0, pl.ds(place, 1), :] = value[:1]
            south_ref[0, pl.ds(place, 1), :] = value[rows - 1 :]
            sides = pack(value, place, lane, sides)
        return sides

    zero = jnp.zeros((rows, cols), jnp.float32)
    west_ref[0], east_ref[0] = lax.fori_loop(0, levels, level, (zero, zero), unroll=2)


def advance_kernel(final, paired, level_ref, mix_ref, *refs):
    x_ref, refs = refs[0], refs[1:]
    base_ref = None
    if paired:
        base_ref, refs = refs[0], refs[1:]
    north_ref, south_ref, west_ref, east_ref, out_ref = refs[:5]
    refs = refs[5:]
    _, variables, levels, rows, cols = x_ref.shape
    lane = lax.broadcasted_iota(jnp.int32, (rows, cols), 1)
    row = lax.broadcasted_iota(jnp.int32, (rows, cols), 0)
    west_halo, east_halo = west_ref[0], east_ref[0]

    def level(l, sides):
        values = [x_ref[0, v, l] for v in range(variables)]
        north_c, south_c, west_c, east_c, centre_c = [level_ref[i, l] for i in range(5)]
        for v in range(variables):
            value, place = values[v], v * levels + l
            north = jnp.where(row == 0, north_ref[0, pl.ds(place, 1), :], pltpu.roll(value, 1, 0))
            south = jnp.where(
                row == rows - 1, south_ref[0, pl.ds(place, 1), :], pltpu.roll(value, rows - 1, 0)
            )
            west = jnp.where(lane == 0, pltpu.roll(west_halo, cols - place, 1), pltpu.roll(value, 1, 1))
            east = jnp.where(
                lane == cols - 1, pltpu.roll(east_halo, cols - 1 - place, 1), pltpu.roll(value, cols - 1, 1)
            )
            change = north_c * north + south_c * south + west_c * west + east_c * east
            change = change + (centre_c + mix_ref[v, v]) * value
            for w in range(variables):
                if w != v:
                    change = change + mix_ref[v, w] * values[w]
            result = value + change
            if paired:
                result = 0.5 * (base_ref[0, v, l] + result)
            if final:
                scratch = refs[0]
                scratch[pl.ds(pl.multiple_of(place * rows, rows), rows), :] = result
            else:
                out_ref[0, v, l] = result
                refs[0][0, pl.ds(place, 1), :] = result[:1]
                refs[1][0, pl.ds(place, 1), :] = result[rows - 1 :]
                sides = pack(result, place, lane, sides)
        return sides

    zero = jnp.zeros((rows, cols), jnp.float32)
    sides = lax.fori_loop(0, levels, level, (zero, zero), unroll=2)
    if not final:
        refs[2][0], refs[3][0] = sides
        return
    groups, width = out_ref.shape[0], out_ref.shape[3]
    for r in range(rows):
        turned = refs[0][pl.ds(r, variables * levels, stride=rows), :].T
        for g in range(groups):
            out_ref[g, 0, r] = turned[g * width : (g + 1) * width]


def edge_specs(shape):
    members, variables, levels, rows, cols = shape
    line = (members, variables * levels, cols)
    side = (members, rows, cols)
    shapes = [jax.ShapeDtypeStruct(d, jnp.float32) for d in (line, line, side, side)]
    specs = [pl.BlockSpec((1,) + d.shape[1:], lambda i: (i, 0, 0)) for d in shapes]
    return shapes, specs


def borders(x):
    shapes, specs = edge_specs(x.shape)
    return pl.pallas_call(
        borders_kernel,
        grid=(x.shape[0],),
        in_specs=[pl.BlockSpec((1,) + x.shape[1:], lambda i: (i, 0, 0, 0, 0))],
        out_specs=specs,
        out_shape=shapes,
        cost_estimate=pl.CostEstimate(flops=x.size * 4, bytes_accessed=x.size * 4, transcendentals=0),
    )(x)


def exchanged(edges):
    north, south, west, east = edges

    def shifted(value, axis, step):
        count = lax.axis_size(axis)
        pairs = [(i, i + 1) for i in range(count - 1)]
        return lax.ppermute(value, axis, pairs if step > 0 else [(j, i) for i, j in pairs])

    return [
        shifted(south, "row", 1),
        shifted(north, "row", -1),
        shifted(east, "col", 1),
        shifted(west, "col", -1),
    ]


def advance(x, base, halos, by_level, mix, final):
    members, variables, levels, rows, cols = x.shape
    shapes, specs = edge_specs(x.shape)
    block = pl.BlockSpec((1,) + x.shape[1:], lambda i: (i, 0, 0, 0, 0))
    scalars = pl.BlockSpec(memory_space=pltpu.SMEM)
    fields = [x] if base is None else [x, base]
    scratch = []
    if final:
        groups = lax.axis_size("mem")
        turned = (groups, members, rows, cols // groups, variables * levels)
        out_shape = [jax.ShapeDtypeStruct(turned, jnp.float32)]
        out_specs = [
            pl.BlockSpec((groups, 1) + turned[2:], lambda i: (0, i, 0, 0, 0))
        ]
        scratch = [pltpu.VMEM((variables * levels * rows, cols), jnp.float32)]
    else:
        out_shape = [jax.ShapeDtypeStruct(x.shape, jnp.float32)] + shapes
        out_specs = [block] + specs
    out = pl.pallas_call(
        lambda *refs: advance_kernel(final, base is not None, *refs),
        grid=(members,),
        in_specs=[scalars, scalars] + [block] * len(fields) + specs,
        out_specs=out_specs,
        out_shape=out_shape,
        scratch_shapes=scratch,
        cost_estimate=pl.CostEstimate(flops=x.size * 40, bytes_accessed=x.size * 12, transcendentals=0),
    )(by_level, mix, *fields, *halos)
    return out[0], out[1:]


def split(value):
    high = value.astype(jnp.bfloat16)
    return high, (value - high.astype(jnp.float32)).astype(jnp.bfloat16)


def doubled(high, low, left):
    both = jnp.where(left, high.astype(jnp.float32), low.astype(jnp.float32)).astype(jnp.bfloat16)
    return jnp.concatenate([both, both], axis=1)


def stacked(high, low):
    return jnp.concatenate([high, high, low, low], axis=0)


def product(left, right):
    return lax.dot_general(left, right, (((1,), (0,)), ((), ())), preferred_element_type=jnp.float32)


def product_t(left, right):
    return lax.dot_general(left, right, (((1,), (1,)), ((), ())), preferred_element_type=jnp.float32)


def analysis_kernel(first_ref, second_ref, index_ref, root_ref, value_ref, out_ref):
    sources, part, count, entries = first_ref.shape
    members = 2 * sources * part
    halves = [ref.reshape(sources * part * count, entries) for ref in (first_ref, second_ref)]
    cells = range(count)
    lane = lax.broadcasted_iota(jnp.int32, (members, 2 * members), 1)
    row = lax.broadcasted_iota(jnp.int32, (members, 2 * members), 0)
    left = lane < members
    left_tall = lax.broadcasted_iota(jnp.int32, (members + 16, 2 * members), 1) < members
    eye = jnp.where((lane == row) | (lane == row + members), 1.0, 0.0).astype(jnp.float32)
    means, perts, systems, gains = [], [], [], []
    for b in cells:
        x = jnp.concatenate([ref[pl.ds(b, sources * part, stride=count), :] for ref in halves], axis=0)
        mean = jnp.sum(x, axis=0, keepdims=True) * (1.0 / members)
        pert = x - mean
        index = jnp.broadcast_to(index_ref[b : b + 1], (members, entries))
        observed = jnp.take_along_axis(pert, index, axis=1)
        obs_mean = jnp.take_along_axis(jnp.broadcast_to(mean, (8, entries)), index[:8], axis=1)
        root = root_ref[b : b + 1]
        innovation = (value_ref[b : b + 1] - obs_mean) * root
        scaled = observed * root
        high, low = split(jnp.concatenate([scaled, innovation, innovation], axis=0))
        ahigh, alow = high[:members], low[:members]
        wide = jnp.concatenate(
            [jnp.concatenate([ahigh, alow], axis=1), jnp.concatenate([ahigh, alow], axis=1)], axis=0
        )
        both = product_t(doubled(high, low, left_tall), wide)
        means.append(mean)
        perts.append(pert)
        systems.append(both[:members] + (members - 1.0) * eye)
        gains.append(both[members : members + 1])
    inverses, rates = [], []
    for b in cells:
        total = 0.5 * jnp.sum(jnp.sum(systems[b] * systems[b], axis=0, keepdims=True), axis=1, keepdims=True)
        rates.append(lax.rsqrt(total))
    for b in cells:
        current = systems[b] * rates[b]
        high, low = split(current)
        square = product(doubled(high, low, left), stacked(high, low))
        shigh, slow = split(square)
        high, low = split(0.0625 * square - 0.5625 * current)
        rest = product(doubled(shigh, slow, left), stacked(high, low))
        inverses.append(2.25 * eye - 2.4375 * current + 1.6875 * square + rest)
    for b in cells:
        high, low = split(inverses[b])
        phigh, plow = split(perts[b])
        moved = product(doubled(high, low, left), stacked(phigh, plow))
        half = 0.5 * jnp.sum(inverses[b] * gains[b], axis=1, keepdims=True)
        shift = jnp.sum(moved * half, axis=0, keepdims=True) * rates[b]
        result = moved * jnp.sqrt((members - 1.0) * rates[b]) + (means[b] + shift)
        for half in range(2):
            for source in range(sources):
                start, at = (half * sources + source) * part, (2 * source + half) * part
                out_ref[b, at : at + part, :] = result[start : start + part]


def analyse(halves, index, value, weight):
    sources, part, cells, entries = halves[0].shape
    members = 2 * sources * part
    count = 8
    small = pl.BlockSpec((count, index.shape[1]), lambda i: (i, 0))
    large = pl.BlockSpec((count, members, entries), lambda i: (i, 0, 0))
    half = pl.BlockSpec((sources, part, count, entries), lambda i: (0, 0, i, 0))
    return pl.pallas_call(
        analysis_kernel,
        grid=(cells // count,),
        in_specs=[half, half, small, small, small],
        out_specs=large,
        out_shape=jax.ShapeDtypeStruct((cells, members, entries), jnp.float32),
    )(*halves, index, jnp.sqrt(weight), value)


def body(
    background_sample,
    coupling,
    diffusion,
    wind_row,
    wind_col,
    observed_entry_index,
    obs_value,
    obs_weight,
):
    members, variables, levels, rows, cols = background_sample.shape
    by_level = jnp.stack(
        [
            diffusion + 0.5 * wind_row,
            diffusion - 0.5 * wind_row,
            diffusion + 0.5 * wind_col,
            diffusion - 0.5 * wind_col,
            -4.0 * diffusion,
        ]
    )
    part = members // PARTS
    states = [background_sample[i * part : (i + 1) * part] for i in range(PARTS)]
    edges = [borders(state) for state in states]
    middles = [None] * PARTS
    for step in range(STEPS):
        last = step == STEPS - 1
        for i in range(PARTS):
            middles[i], edges[i] = advance(
                states[i], None, exchanged(edges[i]), by_level, coupling, False
            )
        for i in range(PARTS):
            states[i], edges[i] = advance(
                middles[i], states[i], exchanged(edges[i]), by_level, coupling, last
            )
    sources = lax.axis_size("mem")
    cells = rows * (cols // sources)
    halves = [
        lax.all_to_all(state, "mem", split_axis=0, concat_axis=0).reshape(
            sources, part, cells, variables * levels
        )
        for state in states
    ]

    def listed(array):
        array = array.reshape(array.shape[0], cells).T
        return jnp.concatenate([array, array], axis=1)

    result = analyse(halves, listed(observed_entry_index), listed(obs_value), listed(obs_weight))
    result = result.transpose(1, 2, 0)
    return result.reshape(result.shape[0], variables, levels, rows, cols // sources)


def solution(mesh):
    placed = (
        P("mem", None, None, "row", "col"),
        P(),
        P(),
        P(),
        P(),
        P(None, "row", ("col", "mem")),
        P(None, "row", ("col", "mem")),
        P(None, "row", ("col", "mem")),
    )
    return jax.shard_map(
        body,
        mesh=mesh,
        in_specs=placed,
        out_specs=P(None, None, None, "row", ("col", "mem")),
        check_vma=False,
    )
```

time: 1600 us -> 781 us (0.49); the launches traced: 1570 us -> 773 us
  local copies, waits for them, and re-layouts: 757 us -> 62.8 us
  Pallas kernels: 65.9 us -> 472 us
  matrix products: 320 us -> 0 us
  other arithmetic: 124 us -> 1.84 us
  waiting for transfers between devices: 249 us -> 137 us
  starting transfers between devices: 56.6 us -> 98.3 us
    pallas_call x1 -> x11, Pallas kernels: 65.9 us -> 472 us  [the longest x8 357 us: advance(): pl.pallas_call(lambda *refs: advance_kernel(final, base is not None, *ref...]
    dot_general x4 -> x0, matrix products: 320 us -> none  [tendency(): jnp.einsum('vw,...wlij->...vlij', coupling, centre, precision=lax.Precisi...]
    slice x16 -> x1, local copies, waits for them, and re-layouts: 273 us -> 11.1 us  [body(): states = [background_sample[i * part:(i + 1) * part] for i in range(PARTS)]]
    unnamed x44 -> x81, local copies, waits for them, and re-layouts: 164 us -> 8.93 us
    ppermute x8 -> x0, local copies, waits for them, and re-layouts: 127 us -> none  [the longest x4 67.1 us: extended(): before = lax.ppermute(last, axis, up)]
    all_to_all x1 -> x2, waiting for transfers between devices: 159 us -> 85.4 us  [body(): lax.all_to_all(state, 'mem', split_axis=0, concat_axis=0)]
    concatenate x3 -> x0, other arithmetic: 61.1 us -> none  [extended(): value = jnp.concatenate([before, value, after], axis=dim)]
    all_to_all x1 -> x0, other arithmetic: 60.7 us -> none  [body(): lax.all_to_all(state, 'mem', split_axis=4, concat_axis=0, tiled=True)]
  transfers between devices with their start and end apart: 17 -> 34, of which waited for: 8 -> 26; matrix products, arithmetic and copies ran while one was open for 10% -> 0% of each run, Pallas kernels for 0% -> 31%
where the time goes in v2:
time: 781 us; the launch traced here: 773 us
  Pallas kernels  472 us (60%)
  waiting for transfers between devices  137 us (18%)
  starting transfers between devices  98.3 us (13%)
  local copies, waits for them, and re-layouts  62.8 us (8%)
    pallas_call x8, Pallas kernels, advance(): pl.pallas_call(lambda *refs: advance_kernel(final, base is not None, *ref...  357 us
    all_to_all x2, waiting for transfers between devices, body(): lax.all_to_all(state, 'mem', split_axis=0, concat_axis=0)  85.4 us
    ppermute x32, starting transfers between devices, shifted(): lax.ppermute(value, axis, pairs if step > 0 else [(j, i) for i, j in pairs])  83.9 us
    pallas_call x1, Pallas kernels, analyse(): pl.pallas_call(analysis_kernel, grid=(cells // count,), in_specs=[half, h...  66.7 us
    ppermute x32, waiting for transfers between devices, shifted(): lax.ppermute(value, axis, pairs if step > 0 else [(j, i) for i, j in pairs])  51.6 us
    pallas_call x2, Pallas kernels, borders(): pl.pallas_call(borders_kernel, grid=(x.shape[0],), in_specs=[pl.BlockSpec...  48.4 us
    reshape x1, local copies, waits for them, and re-layouts, body(): result.reshape(result.shape[0], variables, levels, rows, cols // sources)  24.6 us
    transpose x1, local copies, waits for them, and re-layouts, body(): result = result.transpose(1, 2, 0)  17.5 us
  transfers between devices with their start and end apart: 34, of which 26 were waited for; matrix products, arithmetic and copies ran while one was open for 0% of the time, Pallas kernels for 31%

profile of v2, /device:TPU:25, one launch (start us, length us, event | category | flops | bytes accessed | tf_op | source)
XLA Modules:
  0.0 772.9 jit_solution(133985231230169993)
XLA Ops:
  0.0 11.1 %fusion = (f32[16,4,32,8,128]{4,3,2,1,0:T(8,128)}, f32[16,4,32,8,128]{4,3,2,1,0:T(8,128)}) fusion(f32[32,4,32,8,128]{4,3,2,1,0:T(8,128)} %param.8), kind=kLoop, calls=%fused_computation.8 | loop fusion | bytes 33554432 | tf_op jit(solution)/shard_map/slice | solution.py:274
  11.1 24.2 %shard_map.82 = (f32[16,128,128]{2,1,0:T(8,128)}, f32[16,128,128]{2,1,0:T(8,128)}, f32[16,8,128]{2,1,0:T(8,128)}, f32[16,8,128]{2,1,0:T(8,128)}) custom-call(f32[16,4,32,8,128]{4,3,2,1,0:T(8,128)} %get-tuple-element.82.x_ref.refs_2_.refs_3_), custom_call_target="tpu_custom_call" | custom-call | flops 8388608 | bytes 8388608 | tf_op jit(solution)/shard_map/pallas_call | solution.py:103
  35.3 3.7 collective-permute-start
  39.0 1.9 collective-permute-start.1
  42.2 4.0 collective-permute-start.3
  47.8 3.2 collective-permute-done.refs_3_
  51.0 4.3 collective-permute-done.1.refs_4_
  56.4 47.9 %shard_map.83 = (f32[16,4,32,8,128]{4,3,2,1,0:T(8,128)}, f32[16,128,128]{2,1,0:T(8,128)}, f32[16,128,128]{2,1,0:T(8,128)}, f32[16,8,128]{2,1,0:T(8,128)}, f32[16,8,128]{2,1,0:T(8,128)}) custom-call(f32[5,32]{1,0:T(8,128)} %stack.23.refs_0_, f32[4,4]{1,0:T(4,128)} %refs_1_.15, f32[16,4,32,8,128]{4,3,2,1,0:T(8,128)} %get-tuple-element.82.x_ref.refs_2_.refs_3_, ...), custom_call_target="tpu_custom_call" | custom-call | flops 83886080 | bytes 25165824 | tf_op jit(solution)/shard_map/pallas_call | solution.py:147
  104.3 1.9 collective-permute-start.4
  106.2 2.5 collective-permute-start.5
  110.0 4.0 collective-permute-start.7
  116.0 2.2 collective-permute-done.4.refs_4_
  118.2 4.3 collective-permute-done.5.refs_5_
  123.5 48.6 %shard_map.84 = (f32[16,4,32,8,128]{4,3,2,1,0:T(8,128)}, f32[16,128,128]{2,1,0:T(8,128)}, f32[16,128,128]{2,1,0:T(8,128)}, f32[16,8,128]{2,1,0:T(8,128)}, f32[16,8,128]{2,1,0:T(8,128)}) custom-call(f32[5,32]{1,0:T(8,128)} %stack.23.refs_0_, f32[4,4]{1,0:T(4,128)} %refs_1_.15, f32[16,4,32,8,128]{4,3,2,1,0:T(8,128)} %get-tuple-element.47.refs_2_, ...), custom_call_target="tpu_custom_call" | custom-call | flops 83886080 | bytes 25165824 | tf_op jit(solution)/shard_map/pallas_call | solution.py:147
  172.2 1.9 collective-permute-start.8
  174.1 2.5 collective-permute-start.9
  177.9 4.0 collective-permute-start.11
  183.9 2.2 collective-permute-done.8.refs_3_
  186.1 4.3 collective-permute-done.9.refs_4_
  191.4 47.9 %shard_map.85 = (f32[16,4,32,8,128]{4,3,2,1,0:T(8,128)}, f32[16,128,128]{2,1,0:T(8,128)}, f32[16,128,128]{2,1,0:T(8,128)}, f32[16,8,128]{2,1,0:T(8,128)}, f32[16,8,128]{2,1,0:T(8,128)}) custom-call(f32[5,32]{1,0:T(8,128)} %stack.23.refs_0_, f32[4,4]{1,0:T(4,128)} %refs_1_.15, f32[16,4,32,8,128]{4,3,2,1,0:T(8,128)} %get-tuple-element.52.refs_2_.refs_3_, ...), custom_call_target="tpu_custom_call" | custom-call | flops 83886080 | bytes 25165824 | tf_op jit(solution)/shard_map/pallas_call | solution.py:147
  239.3 1.9 collective-permute-start.12
  241.2 2.5 collective-permute-start.13
  245.0 4.0 collective-permute-start.15
  249.0 24.2 %shard_map.87 = (f32[16,128,128]{2,1,0:T(8,128)}, f32[16,128,128]{2,1,0:T(8,128)}, f32[16,8,128]{2,1,0:T(8,128)}, f32[16,8,128]{2,1,0:T(8,128)}) custom-call(f32[16,4,32,8,128]{4,3,2,1,0:T(8,128)} %get-tuple-element.81.x_ref.refs_2_.refs_3_), custom_call_target="tpu_custom_call" | custom-call | flops 8388608 | bytes 8388608 | tf_op jit(solution)/shard_map/pallas_call | solution.py:103
  273.2 3.6 collective-permute-start.16
  276.9 1.9 collective-permute-start.17
  280.3 34.2 %shard_map.86 = f32[2,16,8,64,128]{4,3,2,1,0:T(8,128)} custom-call(f32[5,32]{1,0:T(8,128)} %stack.23.refs_0_, f32[4,4]{1,0:T(4,128)} %refs_1_.15, f32[16,4,32,8,128]{4,3,2,1,0:T(8,128)} %get-tuple-element.57.refs_2_, f32[16,4,32,8,128]{4,3,2,1,0:T(8,128)} %get-tuple-element.52.refs_2_.refs_3_, f32[16,128,128]{2,1,0:T(8,128)} %copy-done, ...), custom_call_target="tpu_custom_call" | custom-call | flops 83886080 | bytes 25165824 | tf_op jit(solution)/shard_map/pallas_call | solution.py:147
  314.5 7.2 all-to-all-start
  323.1 4.0 collective-permute-start.19
  329.4 47.9 %shard_map.88 = (f32[16,4,32,8,128]{4,3,2,1,0:T(8,128)}, f32[16,128,128]{2,1,0:T(8,128)}, f32[16,128,128]{2,1,0:T(8,128)}, f32[16,8,128]{2,1,0:T(8,128)}, f32[16,8,128]{2,1,0:T(8,128)}) custom-call(f32[5,32]{1,0:T(8,128)} %stack.23.refs_0_, f32[4,4]{1,0:T(4,128)} %refs_1_.15, f32[16,4,32,8,128]{4,3,2,1,0:T(8,128)} %get-tuple-element.81.x_ref.refs_2_.refs_3_, ...), custom_call_target="tpu_custom_call" | custom-call | flops 83886080 | bytes 25165824 | tf_op jit(solution)/shard_map/pallas_call | solution.py:147
  377.3 4.8 collective-permute-start.20
  385.3 4.6 collective-permute-start.23
  391.6 2.6 collective-permute-done.20.refs_4_
  394.1 4.7 collective-permute-done.21.refs_5_
  399.8 48.6 %shard_map.89 = (f32[16,4,32,8,128]{4,3,2,1,0:T(8,128)}, f32[16,128,128]{2,1,0:T(8,128)}, f32[16,128,128]{2,1,0:T(8,128)}, f32[16,8,128]{2,1,0:T(8,128)}, f32[16,8,128]{2,1,0:T(8,128)}) custom-call(f32[5,32]{1,0:T(8,128)} %stack.23.refs_0_, f32[4,4]{1,0:T(4,128)} %refs_1_.15, f32[16,4,32,8,128]{4,3,2,1,0:T(8,128)} %get-tuple-element.66.refs_2_, ...), custom_call_target="tpu_custom_call" | custom-call | flops 83886080 | bytes 25165824 | tf_op jit(solution)/shard_map/pallas_call | solution.py:147
  450.4 2.5 collective-permute-start.25
  454.2 4.6 collective-permute-start.27
  462.4 4.3 collective-permute-done.25.refs_4_
  467.7 47.8 %shard_map.90 = (f32[16,4,32,8,128]{4,3,2,1,0:T(8,128)}, f32[16,128,128]{2,1,0:T(8,128)}, f32[16,128,128]{2,1,0:T(8,128)}, f32[16,8,128]{2,1,0:T(8,128)}, f32[16,8,128]{2,1,0:T(8,128)}) custom-call(f32[5,32]{1,0:T(8,128)} %stack.23.refs_0_, f32[4,4]{1,0:T(4,128)} %refs_1_.15, f32[16,4,32,8,128]{4,3,2,1,0:T(8,128)} %get-tuple-element.71.refs_2_.refs_3_, ...), custom_call_target="tpu_custom_call" | custom-call | flops 83886080 | bytes 25165824 | tf_op jit(solution)/shard_map/pallas_call | solution.py:147
  517.5 2.5 collective-permute-start.29
  521.3 4.6 collective-permute-start.31
  529.6 4.3 collective-permute-done.29.refs_5_
  534.8 34.2 %shard_map.91 = f32[2,16,8,64,128]{4,3,2,1,0:T(8,128)} custom-call(f32[5,32]{1,0:T(8,128)} %stack.23.refs_0_, f32[4,4]{1,0:T(4,128)} %refs_1_.15, f32[16,4,32,8,128]{4,3,2,1,0:T(8,128)} %get-tuple-element.76.refs_2_, f32[16,4,32,8,128]{4,3,2,1,0:T(8,128)} %get-tuple-element.71.refs_2_.refs_3_, f32[16,128,128]{2,1,0:T(8,128)} %copy-done.6, ...), custom_call_target="tpu_custom_call" | custom-call | flops 83886080 | bytes 25165824 | tf_op jit(solution)/shard_map/pallas_call | solution.py:147
  569.1 7.1 all-to-all-start.1
  578.5 85.4 %all-to-all-done.1 = f32[2,16,8,64,128]{4,3,2,1,0:T(8,128)} async-done(((f32[2,16,8,64,128]{4,3,2,1,0:T(8,128)}), f32[2,16,8,64,128]{4,3,2,1,0:T(8,128)}, u32[]{:S(2)}, u32[]{:S(2)}) %all-to-all-start.1) | async-done | bytes 8388640 | tf_op jit(solution)/shard_map/all_to_all | solution.py:290
  664.0 66.7 %shard_map.92 = f32[512,64,128]{2,1,0:T(8,128)} custom-call(f32[2,16,512,128]{3,2,1,0:T(8,128)} %bitcast.5.first_ref, f32[2,16,512,128]{3,2,1,0:T(8,128)} %bitcast.6.second_ref, s32[512,128]{1,0:T(8,128)} %pad_add_fusion.index_ref, f32[512,128]{1,0:T(8,128)} %get-tuple-element.91.root_ref, f32[512,128]{1,0:T(8,128)} %get-tuple-element.92.value_ref), custom_call_target="tpu_custom_call" | custom-call | tf_op jit(solution)/shard_map/pallas_call | solution.py:244
  730.7 17.5 %copy.16 = f32[64,128,512]{2,1,0:T(8,128)} copy(f32[64,128,512]{1,0,2:T(8,128)} %bitcast.22) | data formatting | bytes 33554432 | tf_op jit(solution)/shard_map/transpose | solution.py:301
  748.2 24.6 %reshape.23 = f32[64,4,32,8,64]{4,3,2,1,0:T(8,128)} reshape(f32[64,128,512]{2,1,0:T(8,128)} %copy.16) | data formatting | bytes 33554432 | tf_op jit(solution)/shard_map/reshape | solution.py:302
  (119 shorter events, 42.8 us)
Async XLA Ops:
  11.1 35.1 %copy-start.34 = (f32[32]{0:T(128)S(1)}, f32[32]{0:T(128)}, u32[]{:S(2)}) copy-start(f32[32]{0:T(128)} %param.10) | copy-start | bytes 388
  11.1 35.2 %copy-start.35 = (f32[32]{0:T(128)S(1)}, f32[32]{0:T(128)}, u32[]{:S(2)}) copy-start(f32[32]{0:T(128)} %param.12) | copy-start | bytes 388
  11.1 35.2 %copy-start.36 = (f32[32]{0:T(128)S(1)}, f32[32]{0:T(128)}, u32[]{:S(2)}) copy-start(f32[32]{0:T(128)} %param.11) | copy-start | bytes 388
  35.3 15.7 %collective-permute-start = (f32[16,128,128]{2,1,0:T(8,128)}, f32[16,128,128]{2,1,0:T(8,128)S(1)}, u32[]{:S(2)}, u32[]{:S(2)}) collective-permute-start(f32[16,128,128]{2,1,0:T(8,128)} %get-tuple-element.43), channel_id=1, source_target_pairs={{0,4},{4,8},{8,12},{1,5},{5,9},{9,13},{2,6},{6,10},{10,14},{3,7},{... | collective-permute-start | bytes 3145736 | tf_op jit(solution)/shard_map/ppermute | solution.py:119
  39.0 16.3 %collective-permute-start.1 = (f32[16,128,128]{2,1,0:T(8,128)}, f32[16,128,128]{2,1,0:T(8,128)S(1)}, u32[]{:S(2)}, u32[]{:S(2)}) collective-permute-start(f32[16,128,128]{2,1,0:T(8,128)} %get-tuple-element.44), channel_id=1, source_target_pairs={{4,0},{8,4},{12,8},{5,1},{9,5},{13,9},{6,2},{10,6},{14,10},{7,3},{... | collective-permute-start | bytes 3145736 | tf_op jit(solution)/shard_map/ppermute | solution.py:119
  40.9 5.9 collective-permute-start.2
  42.2 5.6 collective-permute-start.3
  46.9 8.5 %copy-start.18 = (f32[16,8,128]{2,1,0:T(8,128)}, f32[16,8,128]{2,1,0:T(8,128)S(1)}, u32[]{:S(2)}) copy-start(f32[16,8,128]{2,1,0:T(8,128)S(1)} %collective-permute-done.2.refs_5_) | copy-start | bytes 196612
  47.8 7.5 copy-start.20
  104.3 14.0 %collective-permute-start.4 = (f32[16,128,128]{2,1,0:T(8,128)}, f32[16,128,128]{2,1,0:T(8,128)S(1)}, u32[]{:S(2)}, u32[]{:S(2)}) collective-permute-start(f32[16,128,128]{2,1,0:T(8,128)} %get-tuple-element.48), channel_id=1, source_target_pairs={{0,4},{4,8},{8,12},{1,5},{5,9},{9,13},{2,6},{6,10},{10,14},{3,7},{... | collective-permute-start | bytes 3145736 | tf_op jit(solution)/shard_map/ppermute | solution.py:119
  106.2 16.3 %collective-permute-start.5 = (f32[16,128,128]{2,1,0:T(8,128)}, f32[16,128,128]{2,1,0:T(8,128)S(1)}, u32[]{:S(2)}, u32[]{:S(2)}) collective-permute-start(f32[16,128,128]{2,1,0:T(8,128)} %get-tuple-element.49), channel_id=1, source_target_pairs={{4,0},{8,4},{12,8},{5,1},{9,5},{13,9},{6,2},{10,6},{14,10},{7,3},{... | collective-permute-start | bytes 3145736 | tf_op jit(solution)/shard_map/ppermute | solution.py:119
  108.7 5.9 collective-permute-start.6
  110.0 6.1 collective-permute-start.7
  114.6 8.0 %copy-start.22 = (f32[16,8,128]{2,1,0:T(8,128)}, f32[16,8,128]{2,1,0:T(8,128)S(1)}, u32[]{:S(2)}) copy-start(f32[16,8,128]{2,1,0:T(8,128)S(1)} %collective-permute-done.6.refs_6_) | copy-start | bytes 196612
  172.2 14.0 %collective-permute-start.8 = (f32[16,128,128]{2,1,0:T(8,128)}, f32[16,128,128]{2,1,0:T(8,128)S(1)}, u32[]{:S(2)}, u32[]{:S(2)}) collective-permute-start(f32[16,128,128]{2,1,0:T(8,128)} %get-tuple-element.53), channel_id=1, source_target_pairs={{0,4},{4,8},{8,12},{1,5},{5,9},{9,13},{2,6},{6,10},{10,14},{3,7},{... | collective-permute-start | bytes 3145736 | tf_op jit(solution)/shard_map/ppermute | solution.py:119
  174.1 16.3 %collective-permute-start.9 = (f32[16,128,128]{2,1,0:T(8,128)}, f32[16,128,128]{2,1,0:T(8,128)S(1)}, u32[]{:S(2)}, u32[]{:S(2)}) collective-permute-start(f32[16,128,128]{2,1,0:T(8,128)} %get-tuple-element.54), channel_id=1, source_target_pairs={{4,0},{8,4},{12,8},{5,1},{9,5},{13,9},{6,2},{10,6},{14,10},{7,3},{... | collective-permute-start | bytes 3145736 | tf_op jit(solution)/shard_map/ppermute | solution.py:119
  176.6 5.9 collective-permute-start.10
  177.9 6.1 collective-permute-start.11
  182.5 8.0 %copy-start.24 = (f32[16,8,128]{2,1,0:T(8,128)}, f32[16,8,128]{2,1,0:T(8,128)S(1)}, u32[]{:S(2)}) copy-start(f32[16,8,128]{2,1,0:T(8,128)S(1)} %collective-permute-done.10.refs_5_) | copy-start | bytes 196612
  239.3 39.5 %collective-permute-start.12 = (f32[16,128,128]{2,1,0:T(8,128)}, f32[16,128,128]{2,1,0:T(8,128)S(1)}, u32[]{:S(2)}, u32[]{:S(2)}) collective-permute-start(f32[16,128,128]{2,1,0:T(8,128)} %get-tuple-element.58), channel_id=1, source_target_pairs={{0,4},{4,8},{8,12},{1,5},{5,9},{9,13},{2,6},{6,10},{10,14},{3,7},{... | collective-permute-start | bytes 3145736 | tf_op jit(solution)/shard_map/ppermute | solution.py:119
  241.2 37.6 %collective-permute-start.13 = (f32[16,128,128]{2,1,0:T(8,128)}, f32[16,128,128]{2,1,0:T(8,128)S(1)}, u32[]{:S(2)}, u32[]{:S(2)}) collective-permute-start(f32[16,128,128]{2,1,0:T(8,128)} %get-tuple-element.59), channel_id=1, source_target_pairs={{4,0},{8,4},{12,8},{5,1},{9,5},{13,9},{6,2},{10,6},{14,10},{7,3},{... | collective-permute-start | bytes 3145736 | tf_op jit(solution)/shard_map/ppermute | solution.py:119
  243.7 33.2 %collective-permute-start.14 = (f32[16,8,128]{2,1,0:T(8,128)}, f32[16,8,128]{2,1,0:T(8,128)S(1)}, u32[]{:S(2)}, u32[]{:S(2)}) collective-permute-start(f32[16,8,128]{2,1,0:T(8,128)} %get-tuple-element.60), channel_id=1, source_target_pairs={{0,1},{1,2},{2,3},{4,5},{5,6},{6,7},{8,9},{9,10},{10,11},{12,13},{... | collective-permute-start | bytes 196616 | tf_op jit(solution)/shard_map/ppermute | solution.py:119
  245.0 33.8 %collective-permute-start.15 = (f32[16,8,128]{2,1,0:T(8,128)}, f32[16,8,128]{2,1,0:T(8,128)S(1)}, u32[]{:S(2)}, u32[]{:S(2)}) collective-permute-start(f32[16,8,128]{2,1,0:T(8,128)} %get-tuple-element.61), channel_id=1, source_target_pairs={{1,0},{2,1},{3,2},{5,4},{6,5},{7,6},{9,8},{10,9},{11,10},{13,12},{... | collective-permute-start | bytes 196616 | tf_op jit(solution)/shard_map/ppermute | solution.py:119
  273.2 55.2 %collective-permute-start.16 = (f32[16,128,128]{2,1,0:T(8,128)}, f32[16,128,128]{2,1,0:T(8,128)S(1)}, u32[]{:S(2)}, u32[]{:S(2)}) collective-permute-start(f32[16,128,128]{2,1,0:T(8,128)} %get-tuple-element.62), channel_id=1, source_target_pairs={{0,4},{4,8},{8,12},{1,5},{5,9},{9,13},{2,6},{6,10},{10,14},{3,7},{... | collective-permute-start | bytes 3145736 | tf_op jit(solution)/shard_map/ppermute | solution.py:119
  276.9 51.5 %collective-permute-start.17 = (f32[16,128,128]{2,1,0:T(8,128)}, f32[16,128,128]{2,1,0:T(8,128)}, u32[]{:S(2)}, u32[]{:S(2)}) collective-permute-start(f32[16,128,128]{2,1,0:T(8,128)} %get-tuple-element.63), channel_id=1, source_target_pairs={{4,0},{8,4},{12,8},{5,1},{9,5},{13,9},{6,2},{10,6},{14,10},{7,3},{... | collective-permute-start | bytes 3145736 | tf_op jit(solution)/shard_map/ppermute | solution.py:119
  314.5 7.3 copy-start.38
  314.5 8.6 %copy-start.37 = (f32[16,8,128]{2,1,0:T(8,128)S(1)}, f32[16,8,128]{2,1,0:T(8,128)}, u32[]{:S(2)}) copy-start(f32[16,8,128]{2,1,0:T(8,128)} %get-tuple-element.65) | copy-start | bytes 196612
  314.5 254.6 %all-to-all-start = ((f32[2,16,8,64,128]{4,3,2,1,0:T(8,128)}), f32[2,16,8,64,128]{4,3,2,1,0:T(8,128)}, u32[]{:S(2)}, u32[]{:S(2)}) async-start(f32[2,16,8,64,128]{4,3,2,1,0:T(8,128)} %shard_map.86), calls=%async_computation | async-start | bytes 16777216 | tf_op jit(solution)/shard_map/all_to_all | solution.py:290
  321.8 5.4 collective-permute-start.18
  323.1 5.3 collective-permute-start.19
  377.3 16.8 %collective-permute-start.20 = (f32[16,128,128]{2,1,0:T(8,128)}, f32[16,128,128]{2,1,0:T(8,128)S(1)}, u32[]{:S(2)}, u32[]{:S(2)}) collective-permute-start(f32[16,128,128]{2,1,0:T(8,128)} %get-tuple-element.67), channel_id=1, source_target_pairs={{0,4},{4,8},{8,12},{1,5},{5,9},{9,13},{2,6},{6,10},{10,14},{3,7},{... | collective-permute-start | bytes 3145736 | tf_op jit(solution)/shard_map/ppermute | solution.py:119
  382.1 16.7 %collective-permute-start.21 = (f32[16,128,128]{2,1,0:T(8,128)}, f32[16,128,128]{2,1,0:T(8,128)S(1)}, u32[]{:S(2)}, u32[]{:S(2)}) collective-permute-start(f32[16,128,128]{2,1,0:T(8,128)} %get-tuple-element.68), channel_id=1, source_target_pairs={{4,0},{8,4},{12,8},{5,1},{9,5},{13,9},{6,2},{10,6},{14,10},{7,3},{... | collective-permute-start | bytes 3145736 | tf_op jit(solution)/shard_map/ppermute | solution.py:119
  384.0 6.2 collective-permute-start.22
  385.3 6.2 collective-permute-start.23
  390.3 8.6 %copy-start.23 = (f32[16,8,128]{2,1,0:T(8,128)}, f32[16,8,128]{2,1,0:T(8,128)S(1)}, u32[]{:S(2)}) copy-start(f32[16,8,128]{2,1,0:T(8,128)S(1)} %collective-permute-done.22.refs_6_) | copy-start | bytes 196612
  448.5 14.0 %collective-permute-start.24 = (f32[16,128,128]{2,1,0:T(8,128)}, f32[16,128,128]{2,1,0:T(8,128)S(1)}, u32[]{:S(2)}, u32[]{:S(2)}) collective-permute-start(f32[16,128,128]{2,1,0:T(8,128)} %get-tuple-element.72), channel_id=1, source_target_pairs={{0,4},{4,8},{8,12},{1,5},{5,9},{9,13},{2,6},{6,10},{10,14},{3,7},{... | collective-permute-start | bytes 3145736 | tf_op jit(solution)/shard_map/ppermute | solution.py:119
  450.4 16.3 %collective-permute-start.25 = (f32[16,128,128]{2,1,0:T(8,128)}, f32[16,128,128]{2,1,0:T(8,128)S(1)}, u32[]{:S(2)}, u32[]{:S(2)}) collective-permute-start(f32[16,128,128]{2,1,0:T(8,128)} %get-tuple-element.73), channel_id=1, source_target_pairs={{4,0},{8,4},{12,8},{5,1},{9,5},{13,9},{6,2},{10,6},{14,10},{7,3},{... | collective-permute-start | bytes 3145736 | tf_op jit(solution)/shard_map/ppermute | solution.py:119
  452.9 6.1 collective-permute-start.26
  454.2 6.7 collective-permute-start.27
  459.0 7.7 %copy-start.26 = (f32[16,8,128]{2,1,0:T(8,128)}, f32[16,8,128]{2,1,0:T(8,128)S(1)}, u32[]{:S(2)}) copy-start(f32[16,8,128]{2,1,0:T(8,128)S(1)} %collective-permute-done.26.refs_5_) | copy-start | bytes 196612
  515.6 14.0 %collective-permute-start.28 = (f32[16,128,128]{2,1,0:T(8,128)}, f32[16,128,128]{2,1,0:T(8,128)S(1)}, u32[]{:S(2)}, u32[]{:S(2)}) collective-permute-start(f32[16,128,128]{2,1,0:T(8,128)} %get-tuple-element.77), channel_id=1, source_target_pairs={{0,4},{4,8},{8,12},{1,5},{5,9},{9,13},{2,6},{6,10},{10,14},{3,7},{... | collective-permute-start | bytes 3145736 | tf_op jit(solution)/shard_map/ppermute | solution.py:119
  517.5 16.3 %collective-permute-start.29 = (f32[16,128,128]{2,1,0:T(8,128)}, f32[16,128,128]{2,1,0:T(8,128)S(1)}, u32[]{:S(2)}, u32[]{:S(2)}) collective-permute-start(f32[16,128,128]{2,1,0:T(8,128)} %get-tuple-element.78), channel_id=1, source_target_pairs={{4,0},{8,4},{12,8},{5,1},{9,5},{13,9},{6,2},{10,6},{14,10},{7,3},{... | collective-permute-start | bytes 3145736 | tf_op jit(solution)/shard_map/ppermute | solution.py:119
  520.0 6.1 collective-permute-start.30
  521.3 6.7 collective-permute-start.31
  526.1 7.7 %copy-start.29 = (f32[16,8,128]{2,1,0:T(8,128)}, f32[16,8,128]{2,1,0:T(8,128)S(1)}, u32[]{:S(2)}) copy-start(f32[16,8,128]{2,1,0:T(8,128)S(1)} %collective-permute-done.30.refs_6_) | copy-start | bytes 196612
  569.0 7.3 copy-start.16
  569.1 7.5 copy-start.17
  569.1 94.9 %all-to-all-start.1 = ((f32[2,16,8,64,128]{4,3,2,1,0:T(8,128)}), f32[2,16,8,64,128]{4,3,2,1,0:T(8,128)}, u32[]{:S(2)}, u32[]{:S(2)}) async-start(f32[2,16,8,64,128]{4,3,2,1,0:T(8,128)} %shard_map.91), calls=%async_computation.1 | async-start | bytes 16777216 | tf_op jit(solution)/shard_map/all_to_all | solution.py:290
  (25 other events, 79.4 us)
